TPU v7x, 32 devices: a whole 2x2x4 slice. The times are simulated.
32 devices in a mesh: groups: 2 (over y), frame: 8 (over z, x), row: 2 (over core).
Axes of the slice: x: 2, y: 2, z: 4, core: 2. Of those that a mesh axis runs over, the one named last changes fastest.
Arguments:
- latents: bfloat16 [16, 1024, 256], P(('groups', 'frame'), 'row'), parts along dimension 0, may hold values from -8 to 8
- ref_frames: int32 [16, 2], P(('groups', 'frame')), parts along dimension 0, may hold values from 0 to 7, as said below
- windows: int32 [16], P(('groups', 'frame')), parts along dimension 0, may hold values from 1 to 2, as said below
- quant_level: int32 [16], P(('groups', 'frame')), parts along dimension 0, may hold values from 0 to 63
- quant_scale: float32 [64, 256], replicated, may hold values from 0.5 to 2
- shared_proj: bfloat16 [256, 256], replicated, may hold values from -0.375 to 0.375
- value_proj: bfloat16 [256, 256], replicated, may hold values from -0.375 to 0.375
- output_proj: bfloat16 [256, 256], replicated, may hold values from -0.75 to 0.75
- conv_taps: bfloat16 [3, 256, 256], replicated, may hold values from -0.21875 to 0.21875
- cotangent: bfloat16 [16, 1024, 256], P(('groups', 'frame'), 'row'), parts along dimension 0, may hold values from -6 to 6
Outputs:
- coded_latent: bfloat16 [16, 1024, 256], P(('groups', 'frame'), 'row'), parts along dimension 0
- grad_latents: bfloat16 [16, 1024, 256], P(('groups', 'frame'), 'row'), parts along dimension 0
- grad_shared: float32 [512, 256], P('groups'), parts along dimension 0
- grad_values: float32 [512, 256], P('groups'), parts along dimension 0
- grad_output: float32 [512, 256], P('groups'), parts along dimension 0
- grad_taps: float32 [6, 256, 256], P('groups'), parts along dimension 0
There are 2 independent parts, one for each index of `groups`. A program takes and returns all parts, laid end to end along the dimension named above; an argument that names none is the same for every part. Nothing has to cross between parts.
Inputs may be any that keep to these rules, and one draw needn't show every extreme that they name: ref_frames[f, s] differs from f by a power of two no larger than 2 ** 2, and that largest distance occurs. `windows`: some frame has a window of 2 rows.
All inputs are finite; a program needn't handle non-finite values.
Results may differ from a plain program's by a relative error of at most 0.0045.
The roundings to bfloat16 on the way count: a program that leaves them out, or rounds other values in their place, can miss the bound.
Values may be sent and summed in bfloat16 or wider, within the bound.
A program may use at most 128 MiB of HBM per device.

v0:
```python
import math

import jax
import jax.numpy as jnp
from jax import lax
from jax.sharding import PartitionSpec as P

HEADS = 8
DH = 32
COLS = 64
QROWS = 8
WMAX = 2
LEVELS = 3


SCORE_GAIN = 1.5
LAST_DIMS = (((1,), (1,)), ((), ()))
FIRST_DIMS = (((0,), (0,)), ((), ()))


def shifted_2(array, axis, by):
    devices = lax.axis_size(axis)
    pairs = [(i, i + by) for i in range(devices) if 0 <= i + by < devices]
    return lax.ppermute(array, axis, pairs)


def from_partner(value, axis, stride):
    mask = 2**stride
    pairs = [(source, source ^ mask) for source in range(lax.axis_size(axis))]
    return lax.ppermute(value, axis, pairs)


def with_halo(array, sides, width):
    for axis, dim in sides:
        devices, length = (lax.axis_size(axis), array.shape[dim])
        up = [(i, (i + 1) % devices) for i in range(devices - 1)]
        down = [(j, i) for i, j in up]
        last = lax.slice_in_dim(array, length - width, length, axis=dim)
        first = lax.slice_in_dim(array, 0, width, axis=dim)
        before = lax.ppermute(last, axis, up)
        after = lax.ppermute(first, axis, down)
        array = jnp.concatenate([before, array, after], axis=dim)
    return array


def split_heads(block):
    return jnp.transpose(block.reshape(block.shape[0], HEADS, DH), (1, 0, 2))


def merge_heads(block):
    return jnp.transpose(block, (1, 0, 2)).reshape(block.shape[1], HEADS * DH)


def head_weights(query_head, key_head, allowed):
    scores = jnp.dot(query_head, key_head.T, preferred_element_type=jnp.float32) * (
        SCORE_GAIN / math.sqrt(DH)
    )
    scores = jnp.where(allowed, scores, -jnp.inf)
    row_max = jnp.max(scores, axis=1, keepdims=True)
    exp_terms = jnp.where(allowed, jnp.exp(scores - row_max), 0.0)
    return exp_terms / jnp.sum(exp_terms, axis=1, keepdims=True)


def block_forward(query, keys, values, allowed):

    def one_head(head_parts):
        query_head, key_head, value_head = head_parts
        weights = head_weights(query_head, key_head, allowed)
        return jnp.dot(weights.astype(jnp.bfloat16), value_head, preferred_element_type=jnp.float32)

    result = lax.map(one_head, (split_heads(query), split_heads(keys), split_heads(values)))
    return merge_heads(result).astype(jnp.bfloat16)


def block_backward(query, keys, values, allowed, upstream):

    def one_head(head_parts):
        query_head, key_head, value_head, grad_head = head_parts
        weights = head_weights(query_head, key_head, allowed)
        prob = weights.astype(jnp.bfloat16)
        grad_prob = jnp.dot(grad_head, value_head.T, preferred_element_type=jnp.float32)
        value_grad = jnp.dot(prob.T, grad_head, preferred_element_type=jnp.float32)
        row_inner = jnp.sum(weights * grad_prob, axis=1, keepdims=True)
        grad_score = (weights * (grad_prob - row_inner) * (SCORE_GAIN / math.sqrt(DH))).astype(
            jnp.bfloat16
        )
        query_grad = jnp.dot(grad_score, key_head, preferred_element_type=jnp.float32)
        key_grad = jnp.dot(grad_score.T, query_head, preferred_element_type=jnp.float32)
        return (query_grad, key_grad, value_grad)

    query_grad, key_grad, value_grad = lax.map(
        one_head,
        (split_heads(query), split_heads(keys), split_heads(values), split_heads(upstream)),
    )
    return (merge_heads(query_grad), merge_heads(key_grad), merge_heads(value_grad))


def allowed_mask(begin_row, window, total_rows):
    key_span = QROWS + 2 * WMAX
    query_rows = begin_row + jnp.repeat(jnp.arange(QROWS, dtype=jnp.int32), COLS)
    key_rows = jnp.tile(
        jnp.repeat(begin_row - WMAX + jnp.arange(key_span, dtype=jnp.int32), COLS), 2
    )
    nearby = jnp.abs(query_rows[:, None] - key_rows[None, :]) <= window
    inside = (key_rows >= 0) & (key_rows < total_rows)
    return nearby & inside[None, :]


def add_window(summed, addend):
    return summed + addend


def against(left_side, weight):
    return lax.dot_general(left_side, weight, LAST_DIMS, preferred_element_type=jnp.float32)


def cross_rows(left_side, right_side):
    return lax.dot_general(left_side, right_side, FIRST_DIMS, preferred_element_type=jnp.float32)


def exact_against(left_side, weight):
    return lax.dot_general(
        left_side,
        weight.astype(jnp.float32),
        LAST_DIMS,
        precision=lax.Precision.HIGHEST,
        preferred_element_type=jnp.float32,
    )


def exact_cross(left_side, right_side):
    return lax.dot_general(
        left_side.astype(jnp.float32),
        right_side,
        FIRST_DIMS,
        precision=lax.Precision.HIGHEST,
        preferred_element_type=jnp.float32,
    )


def fetch_slots(payload, frame_id, own_refs, offsets):
    slot_data = jnp.zeros((2,) + payload.shape, payload.dtype)
    for offset in offsets:
        arrived = shifted_2(payload, "frame", offset)
        matched = (own_refs == frame_id - offset).reshape((2,) + (1,) * payload.ndim)
        slot_data = jnp.where(matched, arrived[None], slot_data)
    return slot_data


def return_slots(partials, frame_id, own_refs, offsets):
    summed = jnp.zeros(partials.shape[1:], jnp.float32)
    for offset in offsets:
        matched = (own_refs == frame_id - offset).reshape((2,) + (1,) * (partials.ndim - 1))
        outgoing = jnp.sum(jnp.where(matched, partials, 0.0), axis=0)
        summed = summed + shifted_2(outgoing, "frame", -offset)
    return summed


def fold_rims(extended, row_id, rows_dev):
    upper_rim = extended[:, :WMAX]
    middle = extended[:, WMAX : WMAX + rows_dev]
    lower_rim = extended[:, WMAX + rows_dev :]
    outgoing = jnp.where(row_id == 0, lower_rim, upper_rim)
    incoming = from_partner(outgoing.astype(jnp.bfloat16), "row", 0).astype(outgoing.dtype)
    filler = jnp.zeros((extended.shape[0], rows_dev - WMAX) + extended.shape[2:], extended.dtype)
    add_first = jnp.where(row_id == 0, 0.0, incoming)
    add_last = jnp.where(row_id == 0, incoming, 0.0)
    return (
        middle
        + jnp.concatenate([add_first, filler], axis=1)
        + jnp.concatenate([filler, add_last], axis=1)
    )


def local(
    latents,
    ref_frames,
    windows,
    quant_level,
    quant_scale,
    shared_proj,
    value_proj,
    output_proj,
    conv_taps,
    cotangent,
):
    width = latents.shape[2]
    rows_dev = latents.shape[1] // COLS
    total_rows = rows_dev * lax.axis_size("row")
    frame_id = lax.axis_index("frame")
    row_id = lax.axis_index("row")
    first_row = row_id * rows_dev
    own_refs = ref_frames[0]
    window = windows[0]
    key_span = QROWS + 2 * WMAX
    ext_rows = rows_dev + 2 * WMAX
    block_ids = jnp.arange(rows_dev // QROWS, dtype=jnp.int32)
    offsets = [direction * (1 << bit_level) for bit_level in range(LEVELS) for direction in (1, -1)]
    grid_shape = (rows_dev, COLS, width)
    tokens = latents[0]
    queries = jnp.dot(tokens, shared_proj, preferred_element_type=jnp.float32).astype(jnp.bfloat16)
    payload = tokens.reshape(grid_shape)
    extended = with_halo(payload, (("row", 0),), WMAX)
    slot_data = fetch_slots(extended, frame_id, own_refs, offsets)
    slot_flat = slot_data.reshape(-1, width)
    slot_keys = (
        jnp.dot(slot_flat, shared_proj, preferred_element_type=jnp.float32)
        .astype(jnp.bfloat16)
        .reshape(2, ext_rows, COLS, width)
    )
    slot_vals = (
        jnp.dot(slot_flat, value_proj, preferred_element_type=jnp.float32)
        .astype(jnp.bfloat16)
        .reshape(2, ext_rows, COLS, width)
    )
    query_grid = queries.reshape(grid_shape)

    def block_parts(block):
        begin_row = block * QROWS
        query = query_grid.reshape(-1, width)
        key_block = slot_keys.reshape(-1, width)
        value_block = slot_vals.reshape(-1, width)
        allowed = allowed_mask(first_row + begin_row, window, total_rows)
        return (query, key_block, value_block, allowed)

    def forward_block(block):
        query, key_block, value_block, allowed = block_parts(block)
        return block_forward(query, key_block, value_block, allowed)

    mixed_rows = lax.map(forward_block, block_ids).reshape(-1, width)
    residual = tokens.astype(jnp.float32) + jnp.dot(
        mixed_rows, output_proj, preferred_element_type=jnp.float32
    )
    hidden = residual.astype(jnp.bfloat16).reshape(grid_shape)
    hidden_ext = with_halo(hidden, (("row", 0),), 1)
    context = jnp.zeros_like(residual)
    for tap_shift in (-1, 0, 1):
        shifted = hidden_ext[1 + tap_shift : 1 + tap_shift + rows_dev].reshape(-1, width)
        context = context + jnp.dot(
            shifted, conv_taps[tap_shift + 1], preferred_element_type=jnp.float32
        )
    level_ids = jnp.arange(quant_scale.shape[0], dtype=jnp.int32)
    gain_row = jnp.sum(jnp.where((level_ids == quant_level[0])[:, None], quant_scale, 0.0), axis=0)
    coded_latent = ((residual + context) * gain_row[None, :]).astype(jnp.bfloat16)
    grad_z = cotangent[0].astype(jnp.float32) * gain_row[None, :]
    grad_zb = grad_z.astype(jnp.bfloat16)
    grad_ext = with_halo(grad_zb.reshape(grid_shape), (("row", 0),), 1)
    grad_resid = grad_z
    for tap_shift in (-1, 0, 1):
        shifted = grad_ext[1 - tap_shift : 1 - tap_shift + rows_dev].reshape(-1, width)
        grad_resid = grad_resid + against(shifted, conv_taps[tap_shift + 1])
    grad_rb = grad_resid.astype(jnp.bfloat16)
    grad_mixed = against(grad_rb, output_proj).astype(jnp.bfloat16).reshape(grid_shape)

    def backward_block(inner_sums, block):
        query_grad, key_grad, value_grad = inner_sums
        query, key_block, value_block, allowed = block_parts(block)
        begin_row = block * QROWS
        upstream = grad_mixed.reshape(-1, width)
        block_query, block_key, block_value = block_backward(
            query, key_block, value_block, allowed, upstream
        )
        query_grad = block_query.reshape(QROWS, COLS, width)
        key_grad = add_window(key_grad, block_key.reshape(2, key_span, COLS, width))
        value_grad = add_window(value_grad, block_value.reshape(2, key_span, COLS, width))
        return ((query_grad, key_grad, value_grad), None)

    initial = (
        jnp.zeros(grid_shape, jnp.float32),
        jnp.zeros((2, ext_rows, COLS, width), jnp.float32),
        jnp.zeros((2, ext_rows, COLS, width), jnp.float32),
    )
    (query_grad, key_grad, value_grad), _ = lax.scan(backward_block, initial, block_ids)
    query_grad = query_grad.reshape(-1, width)
    flat_keys = key_grad.reshape(-1, width)
    flat_vals = value_grad.reshape(-1, width)
    partials = (
        exact_against(flat_keys, shared_proj) + exact_against(flat_vals, value_proj)
    ).reshape(2, ext_rows, COLS, width)
    returned = fold_rims(
        return_slots(partials, frame_id, own_refs, offsets)[None], row_id, rows_dev
    )[0]
    returned = returned.reshape(-1, returned.shape[-1])
    grad_latents = grad_resid + exact_against(query_grad, shared_proj) + returned
    grad_shared = exact_cross(tokens, query_grad) + exact_cross(slot_flat, flat_keys)
    grad_values = exact_cross(slot_flat, flat_vals)
    grad_output = cross_rows(mixed_rows, grad_rb)
    grad_taps = jnp.stack(
        [
            cross_rows(
                hidden_ext[1 + tap_shift : 1 + tap_shift + rows_dev].reshape(-1, width), grad_zb
            )
            for tap_shift in (-1, 0, 1)
        ]
    )
    grad_shared, grad_values, grad_output, grad_taps = lax.psum(
        (grad_shared, grad_values, grad_output, grad_taps), ("frame", "row")
    )
    norm_scale = 1.0 / math.sqrt(lax.axis_size("frame") * total_rows * COLS)
    return (
        coded_latent.reshape(1, -1, width),
        grad_latents.astype(jnp.bfloat16).reshape(1, -1, width),
        grad_shared * norm_scale,
        grad_values * norm_scale,
        grad_output * norm_scale,
        grad_taps * norm_scale,
    )


def solution(mesh):
    placed = (
        P(("groups", "frame"), "row", None),
        P(("groups", "frame"), None),
        P(("groups", "frame")),
        P(("groups", "frame")),
        P(),
        P(),
        P(),
        P(),
        P(),
        P(("groups", "frame"), "row", None),
    )
    return jax.shard_map(
        local,
        mesh=mesh,
        in_specs=placed,
        out_specs=(
            P(("groups", "frame"), "row", None),
            P(("groups", "frame"), "row", None),
            P("groups", None),
            P("groups", None),
            P("groups", None),
            P("groups", None, None),
        ),
        check_vma=False,
    )
```

profile of v0, /device:TPU:0, one launch (start us, length us, event | category | flops | bytes accessed | tf_op | source)
XLA Modules:
  0.0 488.2 jit_solution(7931116638724330434)
XLA Ops:
  29.3 5.6 %collective-permute-start.7 = (bf16[12,64,256]{2,1,0:T(8,128)(2,1)}, bf16[12,64,256]{2,1,0:T(8,128)(2,1)}, u32[]{:S(2)}, u32[]{:S(2)}) collective-permute-start(bf16[12,64,256]{2,1,0:T(8,128)(2,1)} %pad_maximum_fusion.1), channel_id=1, source_target_pairs={{0,2},{2,4},{4,6},{6,8},{8,10},{10,12},{12,14},{1,3},{3,5},{5,7},{... | collective-permute-start | bytes 1179656 | tf_op jit(solution)/shard_map/ppermute | solution.py:24
  41.8 5.6 %collective-permute-start.5 = (bf16[12,64,256]{2,1,0:T(8,128)(2,1)}, bf16[12,64,256]{2,1,0:T(8,128)(2,1)}, u32[]{:S(2)}, u32[]{:S(2)}) collective-permute-start(bf16[12,64,256]{2,1,0:T(8,128)(2,1)} %pad_maximum_fusion.1), channel_id=1, source_target_pairs={{0,4},{2,6},{4,8},{6,10},{8,12},{10,14},{1,5},{3,7},{5,9},{7,11},{... | collective-permute-start | bytes 1179656 | tf_op jit(solution)/shard_map/ppermute | solution.py:24
  48.7 5.6 %collective-permute-start.3 = (bf16[12,64,256]{2,1,0:T(8,128)(2,1)}, bf16[12,64,256]{2,1,0:T(8,128)(2,1)}, u32[]{:S(2)}, u32[]{:S(2)}) collective-permute-start(bf16[12,64,256]{2,1,0:T(8,128)(2,1)} %pad_maximum_fusion.1), channel_id=1, source_target_pairs={{0,8},{2,10},{4,12},{6,14},{1,9},{3,11},{5,13},{7,15},{16,24},{18,... | collective-permute-start | bytes 1179656 | tf_op jit(solution)/shard_map/ppermute | solution.py:24
  59.3 3.7 collective-permute-done.4
  64.8 16.1 %collective-permute-done.2 = bf16[12,64,256]{2,1,0:T(8,128)(2,1)} collective-permute-done((bf16[12,64,256]{2,1,0:T(8,128)(2,1)}, bf16[12,64,256]{2,1,0:T(8,128)(2,1)}, u32[]{:S(2)}, u32[]{:S(2)}) %collective-permute-start.2) | collective-permute-done | bytes 393248 | tf_op jit(solution)/shard_map/ppermute | solution.py:24
  86.4 3.7 copy.18
  92.8 73.0 %while.46 = (s32[]{:T(128)}, bf16[8,512,32]{1,2,0:T(8,128)(2,1)}, bf16[8,512,32]{2,1,0:T(8,128)(2,1)}, bf16[8,1536,32]{2,1,0:T(8,128)(2,1)}, bf16[8,1536,32]{2,1...) while((s32[]{:T(128)}, bf16[8,512,32]{1,2,0:T(8,128)(2,1)}, ...), condition=%wide.region_3.4_spmd.clone.clone, body=%wide.region_0.3_spmd.clone.sunk.clone | while | flops 117963776 | bytes 10462825 | solution.py:71
  98.1 3.9 fusion.159
  107.2 3.9 fusion.159
  116.3 3.9 fusion.159
  125.4 3.9 fusion.159
  134.6 3.9 fusion.159
  143.7 3.9 fusion.159
  152.8 3.9 fusion.159
  161.9 3.9 fusion.159
  169.8 145.0 %while.47 = (s32[]{:T(128)}, f32[8,512,32]{1,2,0:T(8,128)S(1)}, f32[8,1536,32]{1,2,0:T(8,128)}, f32[8,1536,32]{1,2,0:T(8,128)S(1)}, bf16[8,512,32]{2,1,0:T(8,128...) while((s32[]{:T(128)}, f32[8,512,32]{1,2,0:T(8,128)S(1)}, ...), condition=%wide.region_9.10_spmd.clone.clone, body=%wide.region_5.9_spmd.clone.sunk.clone | while | flops 284686848 | bytes 28981892 | solution.py:91
  178.2 3.5 multiply_reduce_fusion.3
  196.4 3.5 multiply_reduce_fusion.3
  232.6 3.5 multiply_reduce_fusion.3
  250.7 3.5 multiply_reduce_fusion.3
  342.0 6.3 %collective-permute-done.13 = f32[12,64,256]{2,1,0:T(8,128)S(1)} collective-permute-done((f32[12,64,256]{2,1,0:T(8,128)S(1)}, f32[12,64,256]{2,1,0:T(8,128)S(1)}, u32[]{:S(2)}, u32[]{:S(2)}) %collective-permute-start.13) | collective-permute-done | bytes 786464 | tf_op jit(solution)/shard_map/ppermute | solution.py:24
  354.4 20.1 %collective-permute-done.16 = f32[12,64,256]{2,1,0:T(8,128)} collective-permute-done((f32[12,64,256]{2,1,0:T(8,128)}, f32[12,64,256]{2,1,0:T(8,128)}, u32[]{:S(2)}, u32[]{:S(2)}) %collective-permute-start.16) | collective-permute-done | bytes 786464 | tf_op jit(solution)/shard_map/ppermute | solution.py:24
  374.5 11.1 %collective-permute-done.14 = f32[12,64,256]{2,1,0:T(8,128)} collective-permute-done((f32[12,64,256]{2,1,0:T(8,128)}, f32[12,64,256]{2,1,0:T(8,128)}, u32[]{:S(2)}, u32[]{:S(2)}) %collective-permute-start.14) | collective-permute-done | bytes 786464 | tf_op jit(solution)/shard_map/ppermute | solution.py:24
  388.2 85.1 %all-reduce.5.cloned.1.call-done = (f32[256,256]{0,1:T(8,128)}, f32[256,256]{0,1:T(8,128)}, f32[256,256]{0,1:T(8,128)}, f32[3,256,256]{2,1,0:T(8,128)}) async-done(((f32[256,256]{0,1:T(8,128)}, f32[256,256]{0,1:T(8,128)}, f32[256,256]{0,1:T(8,128)}, f32[3,256,256]{2,1,0:T(8,128)}), (f32[256,256]{0,1:T(8,128)}, f32[256,256]{0,1:T(8,128)}, f32[256,256]{0,1:T(8,128)}, ...) | async-done | bytes 1572880 | tf_op jit(solution)/shard_map/psum | solution.py:296
  (225 shorter events, 264.4 us)
Async XLA Ops:
  7.2 21.3 %copy-start.3 = (bf16[1,512,256]{2,1,0:T(8,128)(2,1)S(1)}, bf16[1,512,256]{2,1,0:T(8,128)(2,1)}, u32[]{:S(2)}) copy-start(bf16[1,512,256]{2,1,0:T(8,128)(2,1)} %param.14) | copy-start | bytes 786436
  7.2 466.0 %all-reduce.5.cloned.1.call-start = ((), (), s32[]{:S(2)}) async-start(), calls=%async_computation | async-start | bytes 3145728 | tf_op jit(solution)/shard_map/psum | solution.py:296
  8.2 31.1 %copy-start.1 = (bf16[1,512,256]{2,1,0:T(8,128)(2,1)S(1)}, bf16[1,512,256]{2,1,0:T(8,128)(2,1)}, u32[]{:S(2)}) copy-start(bf16[1,512,256]{2,1,0:T(8,128)(2,1)} %param.23) | copy-start | bytes 786436
  8.2 20.3 %collective-permute-start.1 = (bf16[2,64,256]{2,1,0:T(8,128)(2,1)S(1)}, bf16[2,64,256]{2,1,0:T(8,128)(2,1)S(1)}, u32[]{:S(2)}, u32[]{:S(2)}) collective-permute-start(bf16[2,64,256]{2,1,0:T(8,128)(2,1)S(1)} %bitcast.292), channel_id=1, source_target_pairs={{1,0},{3,2},{5,4},{7,6},{9,8},{11,10},{13,12},{15,14},{17,16},{19,... | collective-permute-start | bytes 196616 | tf_op jit(solution)/shard_map/ppermute | solution.py:41
  9.6 18.9 %collective-permute-start = (bf16[2,64,256]{2,1,0:T(8,128)(2,1)S(1)}, bf16[2,64,256]{2,1,0:T(8,128)(2,1)S(1)}, u32[]{:S(2)}, u32[]{:S(2)}) collective-permute-start(bf16[2,64,256]{2,1,0:T(8,128)(2,1)S(1)} %bitcast.291), channel_id=1, source_target_pairs={{0,1},{2,3},{4,5},{6,7},{8,9},{10,11},{12,13},{14,15},{16,17},{18,... | collective-permute-start | bytes 196616 | tf_op jit(solution)/shard_map/ppermute | solution.py:40
  16.6 21.9 %collective-permute-start.11 = (bf16[1,64,256]{2,1,0:T(8,128)(2,1)}, bf16[1,64,256]{2,1,0:T(8,128)(2,1)}, u32[]{:S(2)}, u32[]{:S(2)}) collective-permute-start(bf16[1,64,256]{2,1,0:T(8,128)(2,1)} %get-tuple-element.261), channel_id=1, source_target_pairs={{0,1},{2,3},{4,5},{6,7},{8,9},{10,11},{12,13},{14,15},{16,17},{18,... | collective-permute-start | bytes 98312 | tf_op jit(solution)/shard_map/ppermute | solution.py:40
  18.5 20.0 %collective-permute-start.10 = (bf16[1,64,256]{2,1,0:T(8,128)(2,1)}, bf16[1,64,256]{2,1,0:T(8,128)(2,1)}, u32[]{:S(2)}, u32[]{:S(2)}) collective-permute-start(bf16[1,64,256]{2,1,0:T(8,128)(2,1)} %get-tuple-element.262), channel_id=1, source_target_pairs={{1,0},{3,2},{5,4},{7,6},{9,8},{11,10},{13,12},{15,14},{17,16},{19,... | collective-permute-start | bytes 98312 | tf_op jit(solution)/shard_map/ppermute | solution.py:41
  29.3 25.0 %collective-permute-start.7 = (bf16[12,64,256]{2,1,0:T(8,128)(2,1)}, bf16[12,64,256]{2,1,0:T(8,128)(2,1)}, u32[]{:S(2)}, u32[]{:S(2)}) collective-permute-start(bf16[12,64,256]{2,1,0:T(8,128)(2,1)} %pad_maximum_fusion.1), channel_id=1, source_target_pairs={{0,2},{2,4},{4,6},{6,8},{8,10},{10,12},{12,14},{1,3},{3,5},{5,7},{... | collective-permute-start | bytes 1179656 | tf_op jit(solution)/shard_map/ppermute | solution.py:24
  40.5 18.7 %collective-permute-start.6 = (bf16[12,64,256]{2,1,0:T(8,128)(2,1)}, bf16[12,64,256]{2,1,0:T(8,128)(2,1)}, u32[]{:S(2)}, u32[]{:S(2)}) collective-permute-start(bf16[12,64,256]{2,1,0:T(8,128)(2,1)} %pad_maximum_fusion.1), channel_id=1, source_target_pairs={{2,0},{4,2},{6,4},{8,6},{10,8},{12,10},{14,12},{3,1},{5,3},{7,5},{... | collective-permute-start | bytes 1179656 | tf_op jit(solution)/shard_map/ppermute | solution.py:24
  41.8 17.4 %collective-permute-start.5 = (bf16[12,64,256]{2,1,0:T(8,128)(2,1)}, bf16[12,64,256]{2,1,0:T(8,128)(2,1)}, u32[]{:S(2)}, u32[]{:S(2)}) collective-permute-start(bf16[12,64,256]{2,1,0:T(8,128)(2,1)} %pad_maximum_fusion.1), channel_id=1, source_target_pairs={{0,4},{2,6},{4,8},{6,10},{8,12},{10,14},{1,5},{3,7},{5,9},{7,11},{... | collective-permute-start | bytes 1179656 | tf_op jit(solution)/shard_map/ppermute | solution.py:24
  47.4 15.6 %collective-permute-start.4 = (bf16[12,64,256]{2,1,0:T(8,128)(2,1)}, bf16[12,64,256]{2,1,0:T(8,128)(2,1)}, u32[]{:S(2)}, u32[]{:S(2)}) collective-permute-start(bf16[12,64,256]{2,1,0:T(8,128)(2,1)} %pad_maximum_fusion.1), channel_id=1, source_target_pairs={{4,0},{6,2},{8,4},{10,6},{12,8},{14,10},{5,1},{7,3},{9,5},{11,7},{... | collective-permute-start | bytes 1179656 | tf_op jit(solution)/shard_map/ppermute | solution.py:24
  48.7 16.1 %collective-permute-start.3 = (bf16[12,64,256]{2,1,0:T(8,128)(2,1)}, bf16[12,64,256]{2,1,0:T(8,128)(2,1)}, u32[]{:S(2)}, u32[]{:S(2)}) collective-permute-start(bf16[12,64,256]{2,1,0:T(8,128)(2,1)} %pad_maximum_fusion.1), channel_id=1, source_target_pairs={{0,8},{2,10},{4,12},{6,14},{1,9},{3,11},{5,13},{7,15},{16,24},{18,... | collective-permute-start | bytes 1179656 | tf_op jit(solution)/shard_map/ppermute | solution.py:24
  54.3 26.6 %collective-permute-start.2 = (bf16[12,64,256]{2,1,0:T(8,128)(2,1)}, bf16[12,64,256]{2,1,0:T(8,128)(2,1)}, u32[]{:S(2)}, u32[]{:S(2)}) collective-permute-start(bf16[12,64,256]{2,1,0:T(8,128)(2,1)} %pad_maximum_fusion.1), channel_id=1, source_target_pairs={{8,0},{10,2},{12,4},{14,6},{9,1},{11,3},{13,5},{15,7},{24,16},{26,... | collective-permute-start | bytes 1179656 | tf_op jit(solution)/shard_map/ppermute | solution.py:24
  92.8 77.0 %copy-start.4 = (f32[8,512,32]{1,2,0:T(8,128)S(1)}, f32[8,512,32]{1,2,0:T(8,128)}, u32[]{:S(2)}) copy-start(f32[8,512,32]{1,2,0:T(8,128)} %custom-call.2) | copy-start | bytes 1572868
  323.2 15.3 %collective-permute-start.8 = (bf16[1,64,256]{2,1,0:T(8,128)(2,1)S(1)}, bf16[1,64,256]{2,1,0:T(8,128)(2,1)S(1)}, u32[]{:S(2)}, u32[]{:S(2)}) collective-permute-start(bf16[1,64,256]{2,1,0:T(8,128)(2,1)S(1)} %get-tuple-element.265), channel_id=1, source_target_pairs={{0,1},{2,3},{4,5},{6,7},{8,9},{10,11},{12,13},{14,15},{16,17},{18,... | collective-permute-start | bytes 98312 | tf_op jit(solution)/shard_map/ppermute | solution.py:40
  325.3 15.3 %collective-permute-start.9 = (bf16[1,64,256]{2,1,0:T(8,128)(2,1)S(1)}, bf16[1,64,256]{2,1,0:T(8,128)(2,1)S(1)}, u32[]{:S(2)}, u32[]{:S(2)}) collective-permute-start(bf16[1,64,256]{2,1,0:T(8,128)(2,1)S(1)} %get-tuple-element.266), channel_id=1, source_target_pairs={{1,0},{3,2},{5,4},{7,6},{9,8},{11,10},{13,12},{15,14},{17,16},{19,... | collective-permute-start | bytes 98312 | tf_op jit(solution)/shard_map/ppermute | solution.py:41
  329.4 18.9 %collective-permute-start.13 = (f32[12,64,256]{2,1,0:T(8,128)S(1)}, f32[12,64,256]{2,1,0:T(8,128)S(1)}, u32[]{:S(2)}, u32[]{:S(2)}) collective-permute-start(f32[12,64,256]{2,1,0:T(8,128)S(1)} %get-tuple-element.201), channel_id=1, source_target_pairs={{0,2},{2,4},{4,6},{6,8},{8,10},{10,12},{12,14},{1,3},{3,5},{5,7},{... | collective-permute-start | bytes 2359304 | tf_op jit(solution)/shard_map/ppermute | solution.py:24
  333.9 20.5 %collective-permute-start.17 = (f32[12,64,256]{2,1,0:T(8,128)}, f32[12,64,256]{2,1,0:T(8,128)}, u32[]{:S(2)}, u32[]{:S(2)}) collective-permute-start(f32[12,64,256]{2,1,0:T(8,128)} %get-tuple-element.202), channel_id=1, source_target_pairs={{0,8},{2,10},{4,12},{6,14},{1,9},{3,11},{5,13},{7,15},{16,24},{18,... | collective-permute-start | bytes 2359304 | tf_op jit(solution)/shard_map/ppermute | solution.py:24
  337.1 37.4 %collective-permute-start.16 = (f32[12,64,256]{2,1,0:T(8,128)}, f32[12,64,256]{2,1,0:T(8,128)}, u32[]{:S(2)}, u32[]{:S(2)}) collective-permute-start(f32[12,64,256]{2,1,0:T(8,128)} %get-tuple-element.203), channel_id=1, source_target_pairs={{8,0},{10,2},{12,4},{14,6},{9,1},{11,3},{13,5},{15,7},{24,16},{26,... | collective-permute-start | bytes 2359304 | tf_op jit(solution)/shard_map/ppermute | solution.py:24
  338.4 36.1 %collective-permute-start.15 = (f32[12,64,256]{2,1,0:T(8,128)}, f32[12,64,256]{2,1,0:T(8,128)}, u32[]{:S(2)}, u32[]{:S(2)}) collective-permute-start(f32[12,64,256]{2,1,0:T(8,128)} %get-tuple-element.204), channel_id=1, source_target_pairs={{0,4},{2,6},{4,8},{6,10},{8,12},{10,14},{1,5},{3,7},{5,9},{7,11},{... | collective-permute-start | bytes 2359304 | tf_op jit(solution)/shard_map/ppermute | solution.py:24
  340.6 44.9 %collective-permute-start.14 = (f32[12,64,256]{2,1,0:T(8,128)}, f32[12,64,256]{2,1,0:T(8,128)}, u32[]{:S(2)}, u32[]{:S(2)}) collective-permute-start(f32[12,64,256]{2,1,0:T(8,128)} %get-tuple-element.205), channel_id=1, source_target_pairs={{4,0},{6,2},{8,4},{10,6},{12,8},{14,10},{5,1},{7,3},{9,5},{11,7},{... | collective-permute-start | bytes 2359304 | tf_op jit(solution)/shard_map/ppermute | solution.py:24
  348.3 37.2 %collective-permute-start.12 = (f32[12,64,256]{2,1,0:T(8,128)}, f32[12,64,256]{2,1,0:T(8,128)}, u32[]{:S(2)}, u32[]{:S(2)}) collective-permute-start(f32[12,64,256]{2,1,0:T(8,128)} %get-tuple-element.206), channel_id=1, source_target_pairs={{2,0},{4,2},{6,4},{8,6},{10,8},{12,10},{14,12},{3,1},{5,3},{7,5},{... | collective-permute-start | bytes 2359304 | tf_op jit(solution)/shard_map/ppermute | solution.py:24
  351.2 34.3 %copy-start.11 = (f32[12,64,256]{2,1,0:T(8,128)S(1)}, f32[12,64,256]{2,1,0:T(8,128)}, u32[]{:S(2)}) copy-start(f32[12,64,256]{2,1,0:T(8,128)} %copy-done.10) | copy-start | bytes 2359300
  388.1 91.9 %collective-permute-start.18 = (bf16[1,2,64,256]{3,2,1,0:T(8,128)(2,1)S(1)}, bf16[1,2,64,256]{3,2,1,0:T(8,128)(2,1)S(1)}, u32[]{:S(2)}, u32[]{:S(2)}) collective-permute-start(bf16[1,2,64,256]{3,2,1,0:T(8,128)(2,1)S(1)} %fusion.70), channel_id=1, source_target_pairs={{0,1},{1,0},{2,3},{3,2},{4,5},{5,4},{6,7},{7,6},{8,9},{9,8},{10,11... | collective-permute-start | bytes 196616 | tf_op jit(solution)/shard_map/ppermute | solution.py:30
  (22 other events, 127.9 us)
Sparse Core Ops, SparseCore 0:
  351.3 121.8 all-reduce.4
where the time goes:
time: 491 us; the launch traced here: 488 us
  matrix products  189 us (38%)
  waiting for transfers between devices  144 us (29%)
  other arithmetic  77 us (16%)
  starting transfers between devices  42.8 us (9%)
  local copies, waits for them, and re-layouts  19.4 us (4%)
  between operations  15.3 us (3%)
    psum x1, waiting for transfers between devices, local(): lax.psum((grad_shared, grad_values, grad_output, grad_taps), ('frame', 'r...  85.1 us
    ppermute x12, waiting for transfers between devices, shifted_2(): return lax.ppermute(array, axis, pairs)  59.2 us
    dot_general x16, matrix products, head_weights(): jnp.dot(query_head, key_head.T, preferred_element_type=jnp.float32)  49.3 us
    reduce_sum x16, other arithmetic, head_weights(): return exp_terms / jnp.sum(exp_terms, axis=1, keepdims=True)  33.9 us
    ppermute x12, starting transfers between devices, shifted_2(): return lax.ppermute(array, axis, pairs)  31.4 us
    dot_general x8, matrix products, one_head(): jnp.dot(weights.astype(jnp.bfloat16), value_head, preferred_element_type=...  31.4 us
    dot_general x8, matrix products, one_head(): jnp.dot(grad_head, value_head.T, preferred_element_type=jnp.float32)  28.1 us
    dot_general x8, matrix products, one_head(): value_grad = jnp.dot(prob.T, grad_head, preferred_element_type=jnp.float32)  25.4 us
  transfers between devices with their start and end apart: 20, of which 8 were waited for; matrix products, arithmetic and copies ran while one was open for 8% of the time, Pallas kernels for 0%

commit v1 on v0

v1 whole, which is shorter than its diff:
```python
import functools
import math

import jax
import jax.numpy as jnp
from jax import lax
from jax.experimental import pallas as pl
from jax.experimental.pallas import tpu as pltpu
from jax.sharding import PartitionSpec as P

HEADS = 8
DH = 32
COLS = 64
QBLK = 4
WMAX = 2
LEVELS = 3

SCORE_SCALE = 1.5 / math.sqrt(DH)
LOG2E = math.log2(math.e)
BF = jnp.bfloat16
F32 = jnp.float32


def mm(a, b, ca=1, cb=0):
    return lax.dot_general(a, b, (((ca,), (cb,)), ((), ())), preferred_element_type=F32)


def attention_kernel(
    bias_ref, q_ref, qt_ref, do_ref, dot_ref, k_ref, v_ref, kt_ref, vt_ref,
    mixt_ref, dqt_ref, dk_ref, dv_ref,
    s_scr, dp_scr, p_scr, ds_scr, qm_scr, dom_scr,
):
    tokens, width = q_ref.shape
    nq = QBLK * COLS
    span = (QBLK + 2 * WMAX) * COLS
    rows = span // COLS
    blocks = tokens // nq
    half = width // 2
    per_half = HEADS // 2
    lane = lax.broadcasted_iota(jnp.int32, (1, width), 1) // DH
    sub = lax.broadcasted_iota(jnp.int32, (half, 1), 0) // DH

    dk_ref[...] = jnp.zeros_like(dk_ref)
    dv_ref[...] = jnp.zeros_like(dv_ref)

    for b in range(blocks):
        q0 = b * nq
        qb = q_ref[q0 : q0 + nq, :]
        dob = do_ref[q0 : q0 + nq, :]
        for h in range(HEADS):
            keep = lane == h
            qm_scr[h * nq : (h + 1) * nq, :] = jnp.where(keep, qb, jnp.zeros_like(qb))
            dom_scr[h * nq : (h + 1) * nq, :] = jnp.where(keep, dob, jnp.zeros_like(dob))

        for hf in range(2):
            f0 = hf * half
            qth = qt_ref[f0 : f0 + half, q0 : q0 + nq]
            doth = dot_ref[f0 : f0 + half, q0 : q0 + nq]

            def one_head(hh, carry, hf=hf, f0=f0, qth=qth, doth=doth, q0=q0, b=b):
                keep = sub == hh
                qtm = jnp.where(keep, qth, jnp.zeros_like(qth))
                dotm = jnp.where(keep, doth, jnp.zeros_like(doth))
                for s in range(2):
                    s_scr[s * span : (s + 1) * span, :] = mm(
                        k_ref[s, q0 : q0 + span, f0 : f0 + half], qtm
                    )
                    dp_scr[s * span : (s + 1) * span, :] = mm(
                        v_ref[s, q0 : q0 + span, f0 : f0 + half], dotm
                    )
                m8 = jnp.full((8, nq), -jnp.inf, F32)
                for c in range(2 * rows):
                    x = s_scr[c * COLS : (c + 1) * COLS, :].reshape(COLS // 8, 8, nq)
                    m8 = jnp.maximum(m8, jnp.max(x, axis=0) + bias_ref[b, c % rows, :][None, :])
                m = jnp.max(m8, axis=0, keepdims=True)
                kk = SCORE_SCALE * LOG2E
                l8 = jnp.zeros((8, nq), F32)
                u8 = jnp.zeros((8, nq), F32)
                for c in range(2 * rows):
                    sl = slice(c * COLS, (c + 1) * COLS)
                    off = (bias_ref[b, c % rows, :][None, :] - m) * kk
                    p = jnp.exp2(s_scr[sl, :] * kk + off)
                    s_scr[sl, :] = p
                    l8 = l8 + jnp.sum(p.reshape(COLS // 8, 8, nq), axis=0)
                    u8 = u8 + jnp.sum((p * dp_scr[sl, :]).reshape(COLS // 8, 8, nq), axis=0)
                inv = 1.0 / jnp.sum(l8, axis=0, keepdims=True)
                ci = inv * SCORE_SCALE
                inner = jnp.sum(u8, axis=0, keepdims=True) * inv * ci
                col = pl.multiple_of((hf * per_half + hh) * nq, nq)
                for c in range(2 * rows):
                    sl = slice(c * COLS, (c + 1) * COLS)
                    p = s_scr[sl, :]
                    p_scr[sl, pl.ds(col, nq)] = (p * inv).astype(BF)
                    ds_scr[sl, pl.ds(col, nq)] = (p * (dp_scr[sl, :] * ci - inner)).astype(BF)
                r0 = pl.multiple_of(f0 + hh * DH, DH)
                mix = jnp.zeros((DH, nq), F32)
                dq = jnp.zeros((DH, nq), F32)
                for s in range(2):
                    ks = slice(s * span, (s + 1) * span)
                    mix = mix + mm(
                        vt_ref[s, pl.ds(r0, DH), q0 : q0 + span], p_scr[ks, pl.ds(col, nq)]
                    )
                    dq = dq + mm(
                        kt_ref[s, pl.ds(r0, DH), q0 : q0 + span], ds_scr[ks, pl.ds(col, nq)]
                    )
                mixt_ref[pl.ds(r0, DH), q0 : q0 + nq] = mix.astype(BF)
                dqt_ref[pl.ds(r0, DH), q0 : q0 + nq] = dq
                return carry

            lax.fori_loop(0, per_half, one_head, 0)

        for s in range(2):
            ks = slice(s * span, (s + 1) * span)
            dk_ref[s, q0 : q0 + span, :] += mm(ds_scr[ks, :], qm_scr[...])
            dv_ref[s, q0 : q0 + span, :] += mm(p_scr[ks, :], dom_scr[...])


def attention(bias, q, qt, do, dot, k, v, kt, vt):
    tokens, width = q.shape
    ext = k.shape[1]
    nq = QBLK * COLS
    keys = 2 * (QBLK + 2 * WMAX) * COLS
    vm = pl.BlockSpec(memory_space=pltpu.VMEM)
    return pl.pallas_call(
        attention_kernel,
        out_shape=(
            jax.ShapeDtypeStruct((width, tokens), BF),
            jax.ShapeDtypeStruct((width, tokens), F32),
            jax.ShapeDtypeStruct((2, ext, width), F32),
            jax.ShapeDtypeStruct((2, ext, width), F32),
        ),
        in_specs=[vm] * 9,
        out_specs=(vm,) * 4,
        scratch_shapes=[
            pltpu.VMEM((keys, nq), F32),
            pltpu.VMEM((keys, nq), F32),
            pltpu.VMEM((keys, HEADS * nq), BF),
            pltpu.VMEM((keys, HEADS * nq), BF),
            pltpu.VMEM((HEADS * nq, width), BF),
            pltpu.VMEM((HEADS * nq, width), BF),
        ],
        compiler_params=pltpu.CompilerParams(vmem_limit_bytes=48 << 20),
        cost_estimate=pl.CostEstimate(
            flops=int(2e10), bytes_accessed=int(8e6), transcendentals=int(4e6)
        ),
        name="attention",
    )(bias, q, qt, do, dot, k, v, kt, vt)


def shifted(array, axis, by):
    devices = lax.axis_size(axis)
    pairs = [(i, i + by) for i in range(devices) if 0 <= i + by < devices]
    return lax.ppermute(array, axis, pairs)


def from_partner(value):
    return lax.ppermute(value, "row", [(0, 1), (1, 0)])


def row_halo(array, row_id, width):
    length = array.shape[-3]
    first = lax.slice_in_dim(array, 0, width, axis=array.ndim - 3)
    last = lax.slice_in_dim(array, length - width, length, axis=array.ndim - 3)
    got = from_partner(jnp.where(row_id == 0, last, first))
    zero = jnp.zeros_like(got)
    before = jnp.where(row_id == 0, zero, got)
    after = jnp.where(row_id == 0, got, zero)
    return jnp.concatenate([before, array, after], axis=array.ndim - 3)


def local(
    latents, ref_frames, windows, quant_level, quant_scale,
    shared_proj, value_proj, output_proj, conv_taps, cotangent,
):
    width = latents.shape[2]
    rows_dev = latents.shape[1] // COLS
    row_devs = lax.axis_size("row")
    total_rows = rows_dev * row_devs
    frame_id = lax.axis_index("frame")
    row_id = lax.axis_index("row")
    own_refs = ref_frames[0]
    window = windows[0]
    ext_rows = rows_dev + 2 * WMAX
    offsets = [d * (1 << level) for level in range(LEVELS) for d in (1, -1)]
    grid = (rows_dev, COLS, width)
    tokens = latents[0]
    token_grid = tokens.reshape(grid)

    slot = jnp.zeros((2,) + grid, BF)
    for offset in offsets:
        arrived = shifted(token_grid, "frame", offset)
        matched = (own_refs == frame_id - offset).reshape(2, 1, 1, 1)
        slot = jnp.where(matched, arrived[None], slot)
    slot_ext = row_halo(slot, row_id, WMAX)
    slot_flat = slot_ext.reshape(2, ext_rows * COLS, width)
    q = mm(tokens, shared_proj).astype(BF)
    qt = mm(shared_proj, tokens, 0, 1).astype(BF)
    k = mm(slot_flat, shared_proj, 2, 0).astype(BF)
    v = mm(slot_flat, value_proj, 2, 0).astype(BF)
    kt = jnp.transpose(k, (0, 2, 1))
    vt = jnp.transpose(v, (0, 2, 1))

    levels = jnp.arange(quant_scale.shape[0], dtype=jnp.int32)
    gain = jnp.sum(jnp.where((levels == quant_level[0])[:, None], quant_scale, 0.0), axis=0)[None]
    grad_z = cotangent[0].astype(F32) * gain
    grad_zb = grad_z.astype(BF)
    grad_ext = row_halo(grad_zb.reshape(grid), row_id, 1).reshape(-1, width)
    grad_resid = grad_z
    for t in range(3):
        part = grad_ext[(2 - t) * COLS : (2 - t + rows_dev) * COLS]
        grad_resid = grad_resid + mm(part, conv_taps[t], 1, 1)
    grad_rb = grad_resid.astype(BF)
    do = mm(grad_rb, output_proj, 1, 1).astype(BF)
    dot = jnp.transpose(do)

    blocks = rows_dev // QBLK
    span_rows = QBLK + 2 * WMAX
    b_i = jnp.arange(blocks, dtype=jnp.int32)[:, None, None]
    r_i = jnp.arange(span_rows, dtype=jnp.int32)[None, :, None]
    i_i = (jnp.arange(QBLK * COLS, dtype=jnp.int32) // COLS)[None, None, :]
    key_row = row_id * rows_dev + b_i * QBLK + r_i - WMAX
    allowed = (jnp.abs(r_i - WMAX - i_i) <= window) & (key_row >= 0) & (key_row < total_rows)
    bias = jnp.where(allowed, 0.0, -jnp.inf).astype(F32)

    mixt, dqt, dk, dv = attention(bias, q, qt, do, dot, k, v, kt, vt)

    residual = tokens.astype(F32) + mm(mixt, output_proj, 0, 0)
    hidden_ext = row_halo(residual.astype(BF).reshape(grid), row_id, 1).reshape(-1, width)
    context = residual
    for t in range(3):
        context = context + mm(hidden_ext[t * COLS : (t + rows_dev) * COLS], conv_taps[t])
    coded = (context * gain).astype(BF)

    dkb = dk.astype(BF)
    dvb = dv.astype(BF)
    partial = (mm(dkb, shared_proj, 2, 1) + mm(dvb, value_proj, 2, 1)).reshape(
        2, ext_rows, COLS, width
    )
    upper = partial[:, :WMAX]
    lower = partial[:, WMAX + rows_dev :]
    got = from_partner(jnp.where(row_id == 0, lower, upper).astype(BF)).astype(F32)
    filler = jnp.zeros((2, rows_dev - WMAX, COLS, width), F32)
    middle = (
        partial[:, WMAX : WMAX + rows_dev]
        + jnp.concatenate([jnp.where(row_id == 0, 0.0, got), filler], axis=1)
        + jnp.concatenate([filler, jnp.where(row_id == 0, got, 0.0)], axis=1)
    )
    grad_latents = grad_resid + mm(dqt.astype(BF), shared_proj, 0, 1)
    for offset in offsets:
        matched = (own_refs == frame_id - offset).reshape(2, 1, 1, 1)
        outgoing = jnp.sum(jnp.where(matched, middle, 0.0), axis=0).astype(BF)
        grad_latents = grad_latents + shifted(outgoing, "frame", -offset).astype(F32).reshape(
            -1, width
        )

    flat = slot_flat.reshape(-1, width)
    grad_shared = mm(tokens, dqt.astype(BF), 0, 1) + mm(flat, dkb.reshape(-1, width), 0, 0)
    grad_values = mm(flat, dvb.reshape(-1, width), 0, 0)
    grad_output = mm(mixt, grad_rb)
    grad_taps = jnp.stack(
        [mm(hidden_ext[t * COLS : (t + rows_dev) * COLS], grad_zb, 0, 0) for t in range(3)]
    )
    sums = lax.psum((grad_shared, grad_values, grad_output, grad_taps), ("frame", "row"))
    norm = 1.0 / math.sqrt(lax.axis_size("frame") * total_rows * COLS)
    return (
        coded[None],
        grad_latents.astype(BF)[None],
        *(total * norm for total in sums),
    )


def solution(mesh):
    tok = P(("groups", "frame"), "row", None)
    frm = P(("groups", "frame"))
    placed = (tok, P(("groups", "frame"), None), frm, frm, P(), P(), P(), P(), P(), tok)
    return jax.shard_map(
        local,
        mesh=mesh,
        in_specs=placed,
        out_specs=(
            tok, tok, P("groups", None), P("groups", None), P("groups", None),
            P("groups", None, None),
        ),
        check_vma=False,
    )
```

time: 491 us -> 213 us (0.43)
  matrix products: 189 us -> 12.9 us
  other arithmetic: 77 us -> 9.64 us
  waiting for transfers between devices: 144 us -> 102 us
  Pallas kernels: 0 us -> 25.1 us
  local copies, waits for them, and re-layouts: 19.4 us -> 10.2 us
  starting transfers between devices: 42.8 us -> 36.5 us
    dot_general x77 -> x22, matrix products: 189 us -> 12.9 us  [mm(): lax.dot_general(a, b, (((ca,), (cb,)), ((), ())), preferred_element_type=...]
    reduce_sum x18 -> x2, other arithmetic: 37.4 us -> 2.46 us  [the longest x1 1.53 us: local(): outgoing = jnp.sum(jnp.where(matched, middle, 0.0), axis=0).astype(BF)]
    ppermute x19 -> x16, waiting for transfers between devices: 59.2 us -> 24.7 us  [the longest x12 24.5 us: shifted(): return lax.ppermute(array, axis, pairs)]
    pallas_call x0 -> x1, Pallas kernels: none -> 25.1 us  [attention(): pl.pallas_call(attention_kernel, out_shape=(jax.ShapeDtypeStruct((width,...]
    convert_element_type x11 -> x5, other arithmetic: 23.4 us -> 1.23 us  [the longest x2 1.05 us: local(): grad_zb = grad_z.astype(BF)]
    another operation x6 -> x0, local copies, waits for them, and re-layouts: 9.24 us -> none  [the longest x4 9.16 us: split_heads(): return jnp.transpose(block.reshape(block.shape[0], HEADS, DH), (1, 0, 2))]
    psum x1, waiting for transfers between devices: 85.1 us -> 77.5 us  [local(): lax.psum((grad_shared, grad_values, grad_output, grad_taps), ('frame', 'r...]
    ppermute x19 -> x16, starting transfers between devices: 42.7 us -> 36.5 us  [the longest x12 35.6 us: shifted(): return lax.ppermute(array, axis, pairs)]
  transfers between devices with their start and end apart: 20 -> 17, of which waited for: 8 -> 7; matrix products, arithmetic and copies ran while one was open for 8% -> 7% of each run, Pallas kernels for 0% -> 0%
where the time goes in v1:
time: 213 us
  waiting for transfers between devices  102 us (48%)
  starting transfers between devices  36.5 us (17%)
  Pallas kernels  25.1 us (12%)
  between operations  16.1 us (8%)
  matrix products  12.9 us (6%)
  local copies, waits for them, and re-layouts  10.2 us (5%)
  other arithmetic  9.64 us (5%)
    psum x1, waiting for transfers between devices, local(): lax.psum((grad_shared, grad_values, grad_output, grad_taps), ('frame', 'r...  77.5 us
    ppermute x12, starting transfers between devices, shifted(): return lax.ppermute(array, axis, pairs)  35.6 us
    pallas_call x1, Pallas kernels, attention(): pl.pallas_call(attention_kernel, out_shape=(jax.ShapeDtypeStruct((width,...  25.1 us
    ppermute x12, waiting for transfers between devices, shifted(): return lax.ppermute(array, axis, pairs)  24.5 us
    dot_general x22, matrix products, mm(): lax.dot_general(a, b, (((ca,), (cb,)), ((), ())), preferred_element_type=...  12.9 us
    unnamed x79, local copies, waits for them, and re-layouts  7.94 us
  transfers between devices with their start and end apart: 17, of which 7 were waited for; matrix products, arithmetic and copies ran while one was open for 7% of the time, Pallas kernels for 0%

profile of v1, /device:TPU:0, one launch (start us, length us, event | category | flops | bytes accessed | tf_op | source)
XLA Modules:
  0.0 212.6 jit_solution(11641132380575369967)
XLA Ops:
  7.3 5.0 %collective-permute-start.6 = (bf16[8,64,256]{2,1,0:T(8,128)(2,1)}, bf16[8,64,256]{2,1,0:T(8,128)(2,1)S(1)}, u32[]{:S(2)}, u32[]{:S(2)}) collective-permute-start(bf16[8,64,256]{2,1,0:T(8,128)(2,1)} %bitcast.147), channel_id=1, source_target_pairs={{0,2},{2,4},{4,6},{6,8},{8,10},{10,12},{12,14},{1,3},{3,5},{5,7},{... | collective-permute-start | bytes 786440 | tf_op jit(solution)/shard_map/ppermute | solution.py:153
  12.3 1.3 collective-permute-start.5
  13.6 6.3 %collective-permute-start.4 = (bf16[8,64,256]{2,1,0:T(8,128)(2,1)}, bf16[8,64,256]{2,1,0:T(8,128)(2,1)}, u32[]{:S(2)}, u32[]{:S(2)}) collective-permute-start(bf16[8,64,256]{2,1,0:T(8,128)(2,1)} %bitcast.149), channel_id=1, source_target_pairs={{0,4},{2,6},{4,8},{6,10},{8,12},{10,14},{1,5},{3,7},{5,9},{7,11},{... | collective-permute-start | bytes 786440 | tf_op jit(solution)/shard_map/ppermute | solution.py:153
  19.8 1.3 collective-permute-start.3
  23.9 1.2 convolution_convert_fusion.4.q_ref
  25.1 1.9 convolution_convert_fusion.3.qt_ref
  28.0 4.9 %collective-permute-start.2 = (bf16[8,64,256]{2,1,0:T(8,128)(2,1)S(1)}, bf16[8,64,256]{2,1,0:T(8,128)(2,1)S(1)}, u32[]{:S(2)}, u32[]{:S(2)}) collective-permute-start(bf16[8,64,256]{2,1,0:T(8,128)(2,1)S(1)} %bitcast.151), channel_id=1, source_target_pairs={{0,8},{2,10},{4,12},{6,14},{1,9},{3,11},{5,13},{7,15},{16,24},{18,... | collective-permute-start | bytes 786440 | tf_op jit(solution)/shard_map/ppermute | solution.py:153
  33.3 1.3 collective-permute-start.1
  35.2 4.0 %collective-permute-done.2 = bf16[8,64,256]{2,1,0:T(8,128)(2,1)S(1)} collective-permute-done((bf16[8,64,256]{2,1,0:T(8,128)(2,1)S(1)}, bf16[8,64,256]{2,1,0:T(8,128)(2,1)S(1)}, u32[]{:S(2)}, u32[]{:S(2)}) %collective-permute-start.2) | collective-permute-done | bytes 262176 | tf_op jit(solution)/shard_map/ppermute | solution.py:153
  39.1 11.0 %collective-permute-done.1 = bf16[8,64,256]{2,1,0:T(8,128)(2,1)S(1)} collective-permute-done((bf16[8,64,256]{2,1,0:T(8,128)(2,1)S(1)}, bf16[8,64,256]{2,1,0:T(8,128)(2,1)S(1)}, u32[]{:S(2)}, u32[]{:S(2)}) %collective-permute-start.1) | collective-permute-done | bytes 262176 | tf_op jit(solution)/shard_map/ppermute | solution.py:153
  50.1 1.4 select_select_fusion
  54.7 1.2 copy.21.v_ref
  58.9 25.1 %attention.1 = (bf16[256,512]{1,0:T(8,128)(2,1)S(1)}, f32[256,512]{1,0:T(8,128)S(1)}, f32[2,768,256]{2,1,0:T(8,128)}, f32[2,768,256]{2,1,0:T(8,128)}) custom-call(f32[2,8,256]{2,1,0:T(8,128)S(1)} %and_select_fusion.bias_ref, bf16[512,256]{1,0:T(8,128)(2,1)S(1)} %convolution_convert_fusion.4.q_ref, bf16[256,512]{1,0:T(8,128)(2,1)S(1)} %copy-done.2, ...), custom_call_target="tpu_custom_call" | custom-call | flops 20000000000 | bytes 8000000 | tf_op jit(solution)/shard_map/attention/pallas_call | solution.py:124
  89.0 1.1 fusion.45
  92.4 1.5 select_reduce_fusion.5
  93.9 1.4 collective-permute-start.10
  96.5 2.2 %collective-permute-start.15 = (bf16[8,64,256]{2,1,0:T(8,128)(2,1)}, bf16[8,64,256]{2,1,0:T(8,128)(2,1)S(1)}, u32[]{:S(2)}, u32[]{:S(2)}) collective-permute-start(bf16[8,64,256]{2,1,0:T(8,128)(2,1)} %get-tuple-element.21), channel_id=1, source_target_pairs={{0,8},{2,10},{4,12},{6,14},{1,9},{3,11},{5,13},{7,15},{16,24},{18,... | collective-permute-start | bytes 786440 | tf_op jit(solution)/shard_map/ppermute | solution.py:153
  98.8 1.3 collective-permute-start.14
  100.1 4.2 %collective-permute-start.13 = (bf16[8,64,256]{2,1,0:T(8,128)(2,1)S(1)}, bf16[8,64,256]{2,1,0:T(8,128)(2,1)S(1)}, u32[]{:S(2)}, u32[]{:S(2)}) collective-permute-start(bf16[8,64,256]{2,1,0:T(8,128)(2,1)S(1)} %get-tuple-element.23), channel_id=1, source_target_pairs={{0,4},{2,6},{4,8},{6,10},{8,12},{10,14},{1,5},{3,7},{5,9},{7,11},{... | collective-permute-start | bytes 786440 | tf_op jit(solution)/shard_map/ppermute | solution.py:153
  104.3 1.3 collective-permute-start.12
  106.0 5.2 %collective-permute-start.11 = (bf16[8,64,256]{2,1,0:T(8,128)(2,1)S(1)}, bf16[8,64,256]{2,1,0:T(8,128)(2,1)S(1)}, u32[]{:S(2)}, u32[]{:S(2)}) collective-permute-start(bf16[8,64,256]{2,1,0:T(8,128)(2,1)S(1)} %get-tuple-element.25), channel_id=1, source_target_pairs={{0,2},{2,4},{4,6},{6,8},{8,10},{10,12},{12,14},{1,3},{3,5},{5,7},{... | collective-permute-start | bytes 786440 | tf_op jit(solution)/shard_map/ppermute | solution.py:153
  112.4 8.8 %collective-permute-done.14 = bf16[8,64,256]{2,1,0:T(8,128)(2,1)S(1)} collective-permute-done((bf16[8,64,256]{2,1,0:T(8,128)(2,1)}, bf16[8,64,256]{2,1,0:T(8,128)(2,1)S(1)}, u32[]{:S(2)}, u32[]{:S(2)}) %collective-permute-start.14) | collective-permute-done | bytes 262176 | tf_op jit(solution)/shard_map/ppermute | solution.py:153
  121.5 1.2 fusion.7
  122.7 77.5 %all-reduce.5.cloned.1.call-done = (f32[256,256]{0,1:T(8,128)}, f32[256,256]{0,1:T(8,128)}, f32[256,256]{0,1:T(8,128)}, f32[3,256,256]{2,1,0:T(8,128)}) async-done(((f32[256,256]{0,1:T(8,128)}, f32[256,256]{0,1:T(8,128)}, f32[256,256]{0,1:T(8,128)}, f32[3,256,256]{2,1,0:T(8,128)}), (f32[256,256]{0,1:T(8,128)}, f32[256,256]{0,1:T(8,128)}, f32[256,256]{0,1:T(8,128)}, ...) | async-done | bytes 1572880 | tf_op jit(solution)/shard_map/psum | solution.py:263
  (146 shorter events, 25.1 us)
Async XLA Ops:
  7.2 193.0 %all-reduce.5.cloned.1.call-start = ((), (), s32[]{:S(2)}) async-start(), calls=%async_computation | async-start | bytes 3145728 | tf_op jit(solution)/shard_map/psum | solution.py:263
  7.3 26.0 %collective-permute-start.6 = (bf16[8,64,256]{2,1,0:T(8,128)(2,1)}, bf16[8,64,256]{2,1,0:T(8,128)(2,1)S(1)}, u32[]{:S(2)}, u32[]{:S(2)}) collective-permute-start(bf16[8,64,256]{2,1,0:T(8,128)(2,1)} %bitcast.147), channel_id=1, source_target_pairs={{0,2},{2,4},{4,6},{6,8},{8,10},{10,12},{12,14},{1,3},{3,5},{5,7},{... | collective-permute-start | bytes 786440 | tf_op jit(solution)/shard_map/ppermute | solution.py:153
  12.3 22.9 %collective-permute-start.5 = (bf16[8,64,256]{2,1,0:T(8,128)(2,1)}, bf16[8,64,256]{2,1,0:T(8,128)(2,1)}, u32[]{:S(2)}, u32[]{:S(2)}) collective-permute-start(bf16[8,64,256]{2,1,0:T(8,128)(2,1)} %bitcast.148), channel_id=1, source_target_pairs={{2,0},{4,2},{6,4},{8,6},{10,8},{12,10},{14,12},{3,1},{5,3},{7,5},{... | collective-permute-start | bytes 786440 | tf_op jit(solution)/shard_map/ppermute | solution.py:153
  13.6 21.6 %collective-permute-start.4 = (bf16[8,64,256]{2,1,0:T(8,128)(2,1)}, bf16[8,64,256]{2,1,0:T(8,128)(2,1)}, u32[]{:S(2)}, u32[]{:S(2)}) collective-permute-start(bf16[8,64,256]{2,1,0:T(8,128)(2,1)} %bitcast.149), channel_id=1, source_target_pairs={{0,4},{2,6},{4,8},{6,10},{8,12},{10,14},{1,5},{3,7},{5,9},{7,11},{... | collective-permute-start | bytes 786440 | tf_op jit(solution)/shard_map/ppermute | solution.py:153
  19.8 15.3 %collective-permute-start.3 = (bf16[8,64,256]{2,1,0:T(8,128)(2,1)}, bf16[8,64,256]{2,1,0:T(8,128)(2,1)}, u32[]{:S(2)}, u32[]{:S(2)}) collective-permute-start(bf16[8,64,256]{2,1,0:T(8,128)(2,1)} %bitcast.150), channel_id=1, source_target_pairs={{4,0},{6,2},{8,4},{10,6},{12,8},{14,10},{5,1},{7,3},{9,5},{11,7},{... | collective-permute-start | bytes 786440 | tf_op jit(solution)/shard_map/ppermute | solution.py:153
  23.8 4.2 %collective-permute-start = (bf16[1,64,256]{2,1,0:T(8,128)(2,1)S(1)}, bf16[1,64,256]{2,1,0:T(8,128)(2,1)S(1)}, u32[]{:S(2)}, u32[]{:S(2)}) collective-permute-start(bf16[1,64,256]{2,1,0:T(8,128)(2,1)S(1)} %fusion.41), channel_id=1, source_target_pairs={{0,1},{1,0},{2,3},{3,2},{4,5},{5,4},{6,7},{7,6},{8,9},{9,8},{10,11... | collective-permute-start | bytes 98312 | tf_op jit(solution)/shard_map/ppermute | solution.py:157
  28.0 22.1 %copy-start.25 = (pred[2]{0:T(512)(128)(4,1)}, pred[2]{0:T(512)(128)(4,1)S(1)}, u32[]{:S(2)}) copy-start(pred[2]{0:T(512)(128)(4,1)S(1)} %get-tuple-element.42) | copy-start | bytes 10
  28.0 22.1 %copy-start.27 = (pred[2]{0:T(512)(128)(4,1)}, pred[2]{0:T(512)(128)(4,1)S(1)}, u32[]{:S(2)}) copy-start(pred[2]{0:T(512)(128)(4,1)S(1)} %get-tuple-element.43) | copy-start | bytes 10
  28.0 22.1 %copy-start.29 = (pred[2]{0:T(512)(128)(4,1)}, pred[2]{0:T(512)(128)(4,1)S(1)}, u32[]{:S(2)}) copy-start(pred[2]{0:T(512)(128)(4,1)S(1)} %get-tuple-element.44) | copy-start | bytes 10
  28.0 11.1 %collective-permute-start.2 = (bf16[8,64,256]{2,1,0:T(8,128)(2,1)S(1)}, bf16[8,64,256]{2,1,0:T(8,128)(2,1)S(1)}, u32[]{:S(2)}, u32[]{:S(2)}) collective-permute-start(bf16[8,64,256]{2,1,0:T(8,128)(2,1)S(1)} %bitcast.151), channel_id=1, source_target_pairs={{0,8},{2,10},{4,12},{6,14},{1,9},{3,11},{5,13},{7,15},{16,24},{18,... | collective-permute-start | bytes 786440 | tf_op jit(solution)/shard_map/ppermute | solution.py:153
  33.3 16.8 %collective-permute-start.1 = (bf16[8,64,256]{2,1,0:T(8,128)(2,1)S(1)}, bf16[8,64,256]{2,1,0:T(8,128)(2,1)S(1)}, u32[]{:S(2)}, u32[]{:S(2)}) collective-permute-start(bf16[8,64,256]{2,1,0:T(8,128)(2,1)S(1)} %bitcast.152), channel_id=1, source_target_pairs={{8,0},{10,2},{12,4},{14,6},{9,1},{11,3},{13,5},{15,7},{24,16},{26,... | collective-permute-start | bytes 786440 | tf_op jit(solution)/shard_map/ppermute | solution.py:153
  51.5 1.4 collective-permute-start.7
  58.9 25.1 %copy-start.9 = (f32[512,256]{1,0:T(8,128)S(1)}, f32[512,256]{1,0:T(8,128)}, u32[]{:S(2)}) copy-start(f32[512,256]{1,0:T(8,128)} %copy-done.8) | copy-start | bytes 1572868
  58.9 26.1 %copy-start.12 = (bf16[1,512,256]{2,1,0:T(8,128)(2,1)S(1)}, bf16[1,512,256]{2,1,0:T(8,128)(2,1)}, u32[]{:S(2)}) copy-start(bf16[1,512,256]{2,1,0:T(8,128)(2,1)} %param.10) | copy-start | bytes 786436
  58.9 26.1 %copy-start.19 = (bf16[256,256]{1,0:T(8,128)(2,1)S(1)}, bf16[256,256]{1,0:T(8,128)(2,1)}, u32[]{:S(2)}) copy-start(bf16[256,256]{1,0:T(8,128)(2,1)} %param.17) | copy-start | bytes 393220
  85.8 5.7 %collective-permute-start.8 = (bf16[1,64,256]{2,1,0:T(8,128)(2,1)S(1)}, bf16[1,64,256]{2,1,0:T(8,128)(2,1)S(1)}, u32[]{:S(2)}, u32[]{:S(2)}) collective-permute-start(bf16[1,64,256]{2,1,0:T(8,128)(2,1)S(1)} %fusion.40), channel_id=1, source_target_pairs={{0,1},{1,0},{2,3},{3,2},{4,5},{5,4},{6,7},{7,6},{8,9},{9,8},{10,11... | collective-permute-start | bytes 98312 | tf_op jit(solution)/shard_map/ppermute | solution.py:157
  88.3 3.9 %collective-permute-start.9 = (bf16[2,2,64,256]{3,2,1,0:T(8,128)(2,1)S(1)}, bf16[2,2,64,256]{3,2,1,0:T(8,128)(2,1)S(1)}, u32[]{:S(2)}, u32[]{:S(2)}) collective-permute-start(bf16[2,2,64,256]{3,2,1,0:T(8,128)(2,1)S(1)} %fusion.8), channel_id=1, source_target_pairs={{0,1},{1,0},{2,3},{3,2},{4,5},{5,4},{6,7},{7,6},{8,9},{9,8},{10,11... | collective-permute-start | bytes 393224 | tf_op jit(solution)/shard_map/ppermute | solution.py:157
  93.9 12.1 %collective-permute-start.10 = (bf16[8,64,256]{2,1,0:T(8,128)(2,1)}, bf16[8,64,256]{2,1,0:T(8,128)(2,1)S(1)}, u32[]{:S(2)}, u32[]{:S(2)}) collective-permute-start(bf16[8,64,256]{2,1,0:T(8,128)(2,1)} %get-tuple-element.20), channel_id=1, source_target_pairs={{2,0},{4,2},{6,4},{8,6},{10,8},{12,10},{14,12},{3,1},{5,3},{7,5},{... | collective-permute-start | bytes 786440 | tf_op jit(solution)/shard_map/ppermute | solution.py:153
  96.5 25.0 %copy-start.10 = (f32[512,256]{1,0:T(8,128)S(1)}, f32[512,256]{1,0:T(8,128)}, u32[]{:S(2)}) copy-start(f32[512,256]{1,0:T(8,128)} %copy-done.8) | copy-start | bytes 1572868
  96.5 15.8 %collective-permute-start.15 = (bf16[8,64,256]{2,1,0:T(8,128)(2,1)}, bf16[8,64,256]{2,1,0:T(8,128)(2,1)S(1)}, u32[]{:S(2)}, u32[]{:S(2)}) collective-permute-start(bf16[8,64,256]{2,1,0:T(8,128)(2,1)} %get-tuple-element.21), channel_id=1, source_target_pairs={{0,8},{2,10},{4,12},{6,14},{1,9},{3,11},{5,13},{7,15},{16,24},{18,... | collective-permute-start | bytes 786440 | tf_op jit(solution)/shard_map/ppermute | solution.py:153
  98.8 22.4 %collective-permute-start.14 = (bf16[8,64,256]{2,1,0:T(8,128)(2,1)}, bf16[8,64,256]{2,1,0:T(8,128)(2,1)S(1)}, u32[]{:S(2)}, u32[]{:S(2)}) collective-permute-start(bf16[8,64,256]{2,1,0:T(8,128)(2,1)} %get-tuple-element.22), channel_id=1, source_target_pairs={{8,0},{10,2},{12,4},{14,6},{9,1},{11,3},{13,5},{15,7},{24,16},{26,... | collective-permute-start | bytes 786440 | tf_op jit(solution)/shard_map/ppermute | solution.py:153
  100.1 21.1 %collective-permute-start.13 = (bf16[8,64,256]{2,1,0:T(8,128)(2,1)S(1)}, bf16[8,64,256]{2,1,0:T(8,128)(2,1)S(1)}, u32[]{:S(2)}, u32[]{:S(2)}) collective-permute-start(bf16[8,64,256]{2,1,0:T(8,128)(2,1)S(1)} %get-tuple-element.23), channel_id=1, source_target_pairs={{0,4},{2,6},{4,8},{6,10},{8,12},{10,14},{1,5},{3,7},{5,9},{7,11},{... | collective-permute-start | bytes 786440 | tf_op jit(solution)/shard_map/ppermute | solution.py:153
  104.3 17.2 %collective-permute-start.12 = (bf16[8,64,256]{2,1,0:T(8,128)(2,1)S(1)}, bf16[8,64,256]{2,1,0:T(8,128)(2,1)S(1)}, u32[]{:S(2)}, u32[]{:S(2)}) collective-permute-start(bf16[8,64,256]{2,1,0:T(8,128)(2,1)S(1)} %copy-done.22), channel_id=1, source_target_pairs={{4,0},{6,2},{8,4},{10,6},{12,8},{14,10},{5,1},{7,3},{9,5},{11,7},{... | collective-permute-start | bytes 786440 | tf_op jit(solution)/shard_map/ppermute | solution.py:153
  106.0 15.5 %collective-permute-start.11 = (bf16[8,64,256]{2,1,0:T(8,128)(2,1)S(1)}, bf16[8,64,256]{2,1,0:T(8,128)(2,1)S(1)}, u32[]{:S(2)}, u32[]{:S(2)}) collective-permute-start(bf16[8,64,256]{2,1,0:T(8,128)(2,1)S(1)} %get-tuple-element.25), channel_id=1, source_target_pairs={{0,2},{2,4},{4,6},{6,8},{8,10},{10,12},{12,14},{1,3},{3,5},{5,7},{... | collective-permute-start | bytes 786440 | tf_op jit(solution)/shard_map/ppermute | solution.py:153
  (31 other events, 233.3 us)
Sparse Core Ops, SparseCore 0:
  96.4 103.7 all-reduce.4

commit v2 on v1

--- a/solution.py
+++ b/solution.py
@@ -13,7 +13,6 @@
 COLS = 64
 QBLK = 4
 WMAX = 2
-LEVELS = 3
 
 SCORE_SCALE = 1.5 / math.sqrt(DH)
 LOG2E = math.log2(math.e)
@@ -147,10 +146,344 @@
     )(bias, q, qt, do, dot, k, v, kt, vt)
 
 
-def shifted(array, axis, by):
-    devices = lax.axis_size(axis)
-    pairs = [(i, i + by) for i in range(devices) if 0 <= i + by < devices]
-    return lax.ppermute(array, axis, pairs)
+MESH = pl.DeviceIdType.MESH
+CHUNKS = 4
+
+
+def greet(targets):
+    barrier = pltpu.get_barrier_semaphore()
+    count = 0
+    for exists, device in targets:
+
+        @pl.when(exists)
+        def _(device=device):
+            pl.semaphore_signal(barrier, inc=1, device_id=device, device_id_type=MESH)
+
+        count = count + jnp.where(exists, 1, 0)
+    pl.semaphore_wait(barrier, count)
+
+
+def fetch_kernel(frames, x_ref, ct_ref, buf_ref, halo_ref, cth_ref, ssem, rsem, hs, hr, cs, cr):
+    f = lax.axis_index("frame")
+    r = lax.axis_index("row")
+    tokens = x_ref.shape[0]
+    odd = lax.rem(f, 2)
+    pair = f + 1 - 2 * odd
+    lo2, hi2, lo4, hi4 = f >= 2, f + 2 < frames, f >= 4, f + 4 < frames
+    side = ((odd == 1) & (f + 1 < frames)) | ((odd == 0) & (f >= 1))
+    always = f >= 0
+    have = (lo2, hi2, always, lo4, hi4, side)
+    partner = {"row": 1 - r}
+    up, down, across = {"frame": f + 2}, {"frame": f - 2}, {"frame": pair}
+    greet(((hi2, up), (lo2, down), (always, across), (always, partner)))
+
+    edge = ct_ref.shape[0] - COLS
+    ct_copy = pltpu.make_async_remote_copy(
+        ct_ref.at[pl.ds(pl.multiple_of((1 - r) * edge, COLS), COLS)], cth_ref, cs, cr,
+        device_id=partner, device_id_type=MESH,
+    )
+    ct_copy.start()
+    step = tokens // CHUNKS
+
+    def copy(kind, c, source, device):
+        part = pl.ds(c * step, step)
+        return pltpu.make_async_remote_copy(
+            source.at[part], buf_ref.at[kind, part], ssem.at[kind, c], rsem.at[kind, c],
+            device_id=device, device_id_type=MESH,
+        )
+
+    for c in range(CHUNKS):
+
+        @pl.when(hi2)
+        def _():
+            copy(0, c, x_ref, up).start()
+
+        @pl.when(lo2)
+        def _():
+            copy(1, c, x_ref, down).start()
+
+        copy(2, c, x_ref, across).start()
+
+    for c in range(CHUNKS):
+
+        @pl.when(lo2)
+        def _():
+            copy(0, c, x_ref, across).wait_recv()
+
+        @pl.when(lo2 & hi2)
+        def _():
+            copy(3, c, buf_ref.at[0], up).start()
+
+        @pl.when(lo2 & (odd == 1))
+        def _():
+            copy(5, c, buf_ref.at[0], across).start()
+
+        @pl.when(hi2)
+        def _():
+            copy(1, c, x_ref, across).wait_recv()
+
+        @pl.when(hi2 & lo2)
+        def _():
+            copy(4, c, buf_ref.at[1], down).start()
+
+        @pl.when(hi2 & (odd == 0))
+        def _():
+            copy(5, c, buf_ref.at[1], across).start()
+
+    rim = WMAX * COLS
+    start = pl.multiple_of((1 - r) * (tokens - rim), rim)
+
+    def halo(kind):
+        return pltpu.make_async_remote_copy(
+            buf_ref.at[kind, pl.ds(start, rim)], halo_ref.at[kind], hs.at[kind], hr.at[kind],
+            device_id=partner, device_id_type=MESH,
+        )
+
+    for kind in range(6):
+
+        @pl.when(have[kind])
+        def _():
+            if kind > 1:
+                for c in range(CHUNKS):
+                    copy(kind, c, x_ref, across).wait_recv()
+            halo(kind).start()
+
+    sent = (hi2, lo2, always, lo2 & hi2, lo2 & hi2, (lo2 & (odd == 1)) | (hi2 & (odd == 0)))
+    for kind in range(6):
+
+        @pl.when(have[kind])
+        def _():
+            halo(kind).wait()
+
+        @pl.when(sent[kind])
+        def _():
+            for c in range(CHUNKS):
+                copy(kind, c, x_ref, across).wait_send()
+
+    ct_copy.wait()
+
+
+def fetch(tokens, cotangent, frames):
+    count, width = tokens.shape
+    vm = pl.BlockSpec(memory_space=pltpu.VMEM)
+    dma = pltpu.SemaphoreType.DMA
+    return pl.pallas_call(
+        functools.partial(fetch_kernel, frames),
+        out_shape=(
+            jax.ShapeDtypeStruct((6, count, width), BF),
+            jax.ShapeDtypeStruct((6, WMAX * COLS, width), BF),
+            jax.ShapeDtypeStruct((COLS, width), BF),
+        ),
+        in_specs=[vm] * 2,
+        out_specs=(vm,) * 3,
+        scratch_shapes=[
+            dma((6, CHUNKS)), dma((6, CHUNKS)), dma((6,)), dma((6,)), dma(()), dma(()),
+        ],
+        compiler_params=pltpu.CompilerParams(collective_id=0, has_side_effects=True),
+        name="fetch",
+    )(tokens, cotangent)
+
+
+def reduce_kernel(
+    frames, out_ref, base_ref, w_ref, lat_ref, wsum_ref,
+    rb, sb, wp, ws, wr, ssem, rsem, ps, pr, rs_s, rs_r, ag_s, ag_r, fw_s, fw_r,
+):
+    f = lax.axis_index("frame")
+    r = lax.axis_index("row")
+    tokens = base_ref.shape[0]
+    odd = lax.rem(f, 2)
+    pair = f + 1 - 2 * odd
+    lo2, hi2, lo4, hi4 = f >= 2, f + 2 < frames, f >= 4, f + 4 < frames
+    always = f >= 0
+    side = ((odd == 1) & (f + 1 < frames)) | ((odd == 0) & (f >= 1))
+    relay = ((odd == 1) & lo2) | ((odd == 0) & hi2)
+    partner = {"row": 1 - r}
+    up, down, across = {"frame": f + 2}, {"frame": f - 2}, {"frame": pair}
+
+    barrier = pltpu.get_barrier_semaphore()
+    pl.semaphore_signal(barrier, inc=1, device_id=partner, device_id_type=MESH)
+
+    def hello(k, carry):
+        pl.semaphore_signal(
+            barrier, inc=1, device_id={"frame": lax.rem(f + k, frames)}, device_id_type=MESH
+        )
+        return carry
+
+    lax.fori_loop(1, frames, hello, 0)
+    pl.semaphore_wait(barrier, frames)
+
+    step = tokens // CHUNKS
+    sent = (hi2, lo2, always, hi4, lo4, side)
+    got = (lo2, hi2, always, lo2 & hi2, lo2 & hi2, relay)
+    device = (up, down, across, up, down, across)
+
+    def copy(kind, c, source):
+        part = pl.ds(c * step, step)
+        return pltpu.make_async_remote_copy(
+            source.at[part], rb.at[kind, part], ssem.at[kind, c], rsem.at[kind, c],
+            device_id=device[kind], device_id_type=MESH,
+        )
+
+    halves = pltpu.make_async_remote_copy(
+        w_ref.at[1 - r], wp, ps, pr, device_id=partner, device_id_type=MESH
+    )
+    halves.start()
+    for c in range(CHUNKS):
+        for kind in (3, 4, 5):
+
+            @pl.when(sent[kind])
+            def _():
+                copy(kind, c, out_ref.at[kind]).start()
+
+    for kind in (0, 1, 3, 4, 5):
+
+        @pl.when(jnp.logical_not(got[kind]))
+        def _():
+            rb[kind, :, :] = jnp.zeros((tokens, rb.shape[2]), BF)
+
+    halves.wait()
+    ws[...] = (w_ref[r] + wp[...]).astype(BF)
+
+    def piece(ref, mine, other, target, s_sem, r_sem, slot, k):
+        return pltpu.make_async_remote_copy(
+            mine, other, s_sem.at[k], r_sem.at[slot],
+            device_id={"frame": target}, device_id_type=MESH,
+        )
+
+    def scatter(k):
+        target = lax.rem(f + k, frames)
+        return piece(ws, ws.at[target], wr.at[f], target, rs_s, rs_r, f, k)
+
+    def arrived(k):
+        source = lax.rem(f - k + frames, frames)
+        return source, piece(ws, ws.at[source], wr.at[source], source, rs_s, rs_r, source, k)
+
+    def gather(k):
+        target = lax.rem(f + k, frames)
+        return piece(ws, wsum_ref.at[r, f], wsum_ref.at[r, f], target, ag_s, ag_r, f, k)
+
+    def gathered(k):
+        source = lax.rem(f - k + frames, frames)
+        return source, piece(
+            ws, wsum_ref.at[r, source], wsum_ref.at[r, source], source, ag_s, ag_r, source, k
+        )
+
+    def forward(j, own):
+        return pltpu.make_async_remote_copy(
+            wsum_ref.at[own, j], wsum_ref.at[own, j], fw_s.at[j], fw_r.at[j],
+            device_id=partner, device_id_type=MESH,
+        )
+
+    def run(body):
+        lax.fori_loop(1, frames, lambda k, carry: (body(k), carry)[1], 0)
+
+    run(lambda k: scatter(k).start())
+    for c in range(CHUNKS):
+        copy(2, c, out_ref.at[2]).start()
+
+    even = jnp.where(odd == 0, 1.0, 0.0).astype(F32)
+    for c in range(CHUNKS):
+        part = slice(c * step, (c + 1) * step)
+        for kind in (3, 4, 5):
+
+            @pl.when(got[kind])
+            def _():
+                copy(kind, c, out_ref.at[kind]).wait_recv()
+
+        extra = rb[5, part, :].astype(F32)
+        rising = out_ref[0, part, :].astype(F32) + rb[3, part, :].astype(F32) + extra * even
+        falling = (
+            out_ref[1, part, :].astype(F32) + rb[4, part, :].astype(F32) + extra * (1.0 - even)
+        )
+        sb[0, part, :] = rising.astype(BF)
+        sb[1, part, :] = falling.astype(BF)
+
+        @pl.when(hi2)
+        def _():
+            copy(0, c, sb.at[0]).start()
+
+        @pl.when(lo2)
+        def _():
+            copy(1, c, sb.at[1]).start()
+
+    def add_piece(k, total):
+        source, waiting = arrived(k)
+        waiting.wait_recv()
+        return total + wr[source].astype(F32)
+
+    total = lax.fori_loop(1, frames, add_piece, w_ref[r, f] + wp[f])
+    wsum_ref[r, f] = total.astype(BF)
+    run(lambda k: gather(k).start())
+    forward(f, r).start()
+
+    for c in range(CHUNKS):
+        part = slice(c * step, (c + 1) * step)
+        for kind in (0, 1, 2):
+
+            @pl.when(got[kind])
+            def _():
+                copy(kind, c, out_ref.at[kind]).wait_recv()
+
+        lat_ref[part, :] = (
+            base_ref[part, :]
+            + rb[0, part, :].astype(F32)
+            + rb[1, part, :].astype(F32)
+            + rb[2, part, :].astype(F32)
+        ).astype(BF)
+
+    def pass_on(k):
+        source, waiting = gathered(k)
+        waiting.wait_recv()
+        forward(source, r).start()
+
+    run(pass_on)
+
+    def finish(k):
+        scatter(k).wait_send()
+        gather(k).wait_send()
+
+    run(finish)
+
+    def last(j, carry):
+        forward(j, r).wait_send()
+        forward(j, 1 - r).wait_recv()
+        return carry
+
+    lax.fori_loop(0, frames, last, 0)
+    for kind in range(6):
+
+        @pl.when(sent[kind])
+        def _():
+            for c in range(CHUNKS):
+                copy(kind, c, out_ref.at[kind]).wait_send()
+
+
+def reduce(outgoing, base, grads, frames):
+    count, width = base.shape
+    vm = pl.BlockSpec(memory_space=pltpu.VMEM)
+    dma = pltpu.SemaphoreType.DMA
+    pieces = grads.shape[1:]
+    return pl.pallas_call(
+        functools.partial(reduce_kernel, frames),
+        out_shape=(
+            jax.ShapeDtypeStruct((count, width), BF),
+            jax.ShapeDtypeStruct(grads.shape, BF),
+        ),
+        in_specs=[vm] * 3,
+        out_specs=(vm,) * 2,
+        scratch_shapes=[
+            pltpu.VMEM((6, count, width), BF),
+            pltpu.VMEM((2, count, width), BF),
+            pltpu.VMEM(pieces, F32),
+            pltpu.VMEM(pieces, BF),
+            pltpu.VMEM(pieces, BF),
+            dma((6, CHUNKS)), dma((6, CHUNKS)), dma(()), dma(()),
+            dma((frames,)), dma((frames,)), dma((frames,)), dma((frames,)),
+            dma((frames,)), dma((frames,)),
+        ],
+        compiler_params=pltpu.CompilerParams(collective_id=1, has_side_effects=True),
+        name="reduce",
+    )(outgoing, base, grads)
 
 
 def from_partner(value):
@@ -181,17 +514,25 @@
     own_refs = ref_frames[0]
     window = windows[0]
     ext_rows = rows_dev + 2 * WMAX
-    offsets = [d * (1 << level) for level in range(LEVELS) for d in (1, -1)]
     grid = (rows_dev, COLS, width)
     tokens = latents[0]
-    token_grid = tokens.reshape(grid)
-
-    slot = jnp.zeros((2,) + grid, BF)
-    for offset in offsets:
-        arrived = shifted(token_grid, "frame", offset)
-        matched = (own_refs == frame_id - offset).reshape(2, 1, 1, 1)
-        slot = jnp.where(matched, arrived[None], slot)
-    slot_ext = row_halo(slot, row_id, WMAX)
+    frames = lax.axis_size("frame")
+    odd = frame_id % 2
+    sources = (
+        frame_id - 2, frame_id + 2, frame_id + 1 - 2 * odd,
+        frame_id - 4, frame_id + 4, frame_id - 1 + 2 * odd,
+    )
+    buf, halo, ct_edge = fetch(tokens, cotangent[0], frames)
+    slot = jnp.zeros((2,) + tokens.shape, BF)
+    rim = jnp.zeros((2, WMAX * COLS, width), BF)
+    for kind, source in enumerate(sources):
+        matched = (own_refs == source).reshape(2, 1, 1)
+        slot = jnp.where(matched, buf[kind][None], slot)
+        rim = jnp.where(matched, halo[kind][None], rim)
+    zero = jnp.zeros_like(rim)
+    slot_ext = jnp.concatenate(
+        [jnp.where(row_id == 0, zero, rim), slot, jnp.where(row_id == 0, rim, zero)], axis=1
+    )
     slot_flat = slot_ext.reshape(2, ext_rows * COLS, width)
     q = mm(tokens, shared_proj).astype(BF)
     qt = mm(shared_proj, tokens, 0, 1).astype(BF)
@@ -204,7 +545,11 @@
     gain = jnp.sum(jnp.where((levels == quant_level[0])[:, None], quant_scale, 0.0), axis=0)[None]
     grad_z = cotangent[0].astype(F32) * gain
     grad_zb = grad_z.astype(BF)
-    grad_ext = row_halo(grad_zb.reshape(grid), row_id, 1).reshape(-1, width)
+    edge = (ct_edge.astype(F32) * gain).astype(BF)
+    blank = jnp.zeros_like(edge)
+    grad_ext = jnp.concatenate(
+        [jnp.where(row_id == 0, blank, edge), grad_zb, jnp.where(row_id == 0, edge, blank)], axis=0
+    )
     grad_resid = grad_z
     for t in range(3):
         part = grad_ext[(2 - t) * COLS : (2 - t + rows_dev) * COLS]
@@ -246,13 +591,18 @@
         + jnp.concatenate([filler, jnp.where(row_id == 0, got, 0.0)], axis=1)
     )
     grad_latents = grad_resid + mm(dqt.astype(BF), shared_proj, 0, 1)
-    for offset in offsets:
-        matched = (own_refs == frame_id - offset).reshape(2, 1, 1, 1)
-        outgoing = jnp.sum(jnp.where(matched, middle, 0.0), axis=0).astype(BF)
-        grad_latents = grad_latents + shifted(outgoing, "frame", -offset).astype(F32).reshape(
-            -1, width
-        )
-
+    targets = (
+        frame_id + 2, frame_id - 2, frame_id + 1 - 2 * odd,
+        frame_id + 4, frame_id - 4, frame_id - 1 + 2 * odd,
+    )
+    outgoing = jnp.stack(
+        [
+            jnp.sum(jnp.where((own_refs == t).reshape(2, 1, 1, 1), middle, 0.0), axis=0)
+            .astype(BF)
+            .reshape(-1, width)
+            for t in targets
+        ]
+    )
     flat = slot_flat.reshape(-1, width)
     grad_shared = mm(tokens, dqt.astype(BF), 0, 1) + mm(flat, dkb.reshape(-1, width), 0, 0)
     grad_values = mm(flat, dvb.reshape(-1, width), 0, 0)
@@ -260,12 +610,20 @@
     grad_taps = jnp.stack(
         [mm(hidden_ext[t * COLS : (t + rows_dev) * COLS], grad_zb, 0, 0) for t in range(3)]
     )
-    sums = lax.psum((grad_shared, grad_values, grad_output, grad_taps), ("frame", "row"))
-    norm = 1.0 / math.sqrt(lax.axis_size("frame") * total_rows * COLS)
+    stacked = jnp.concatenate(
+        [grad_shared, grad_values, grad_output, grad_taps.reshape(-1, width)], axis=0
+    )
+    grads = stacked.reshape(2, frames, stacked.shape[0] // (2 * frames), width)
+    new_latents, summed = reduce(outgoing, grad_latents, grads, frames)
+    norm = 1.0 / math.sqrt(frames * total_rows * COLS)
+    summed = summed.reshape(-1, width).astype(F32) * norm
     return (
         coded[None],
-        grad_latents.astype(BF)[None],
-        *(total * norm for total in sums),
+        new_latents[None],
+        summed[:width],
+        summed[width : 2 * width],
+        summed[2 * width : 3 * width],
+        summed[3 * width :].reshape(3, width, width),
     )
 
 

time: 213 us -> 118 us (0.55)
  waiting for transfers between devices: 102 us -> 0.01 us
  Pallas kernels: 25.1 us -> 81.2 us
  starting transfers between devices: 36.5 us -> 0.85 us
  between operations: 16.1 us -> 2.65 us
    psum x1 -> x0, waiting for transfers between devices: 77.5 us -> none  [local(): lax.psum((grad_shared, grad_values, grad_output, grad_taps), ('frame', 'r...]
    pallas_call x0 -> x2, Pallas kernels: none -> 56.1 us  [the longest x1 35.9 us: reduce(): pl.pallas_call(functools.partial(reduce_kernel, frames), out_shape=(jax.S...]
    ppermute x12 -> x0, starting transfers between devices: 35.6 us -> none  [shifted(): return lax.ppermute(array, axis, pairs)]
    ppermute x12 -> x0, waiting for transfers between devices: 24.5 us -> none  [shifted(): return lax.ppermute(array, axis, pairs)]
    unnamed x79 -> x74, local copies, waits for them, and re-layouts: 7.94 us -> 6.95 us
  transfers between devices with their start and end apart: 17 -> 2, of which waited for: 7 -> 0; matrix products, arithmetic and copies ran while one was open for 7% -> 5% of each run, Pallas kernels for 0% -> 0%
where the time goes in v2:
time: 118 us
  Pallas kernels  81.2 us (69%)
  matrix products  12.8 us (11%)
  local copies, waits for them, and re-layouts  11.3 us (10%)
  other arithmetic  8.71 us (7%)
  between operations  2.65 us (2%)
    pallas_call x1, Pallas kernels, reduce(): pl.pallas_call(functools.partial(reduce_kernel, frames), out_shape=(jax.S...  35.9 us
    pallas_call x1, Pallas kernels, attention(): pl.pallas_call(attention_kernel, out_shape=(jax.ShapeDtypeStruct((width,...  25.1 us
    pallas_call x1, Pallas kernels, fetch(): pl.pallas_call(functools.partial(fetch_kernel, frames), out_shape=(jax.Sh...  20.1 us
    dot_general x22, matrix products, mm(): lax.dot_general(a, b, (((ca,), (cb,)), ((), ())), preferred_element_type=...  12.8 us
    unnamed x74, local copies, waits for them, and re-layouts  6.95 us
  transfers between devices with their start and end apart: 2, of which 0 were waited for; matrix products, arithmetic and copies ran while one was open for 5% of the time, Pallas kernels for 0%

profile of v2, /device:TPU:0, one launch (start us, length us, event | category | flops | bytes accessed | tf_op | source)
XLA Modules:
  0.0 117.5 jit_solution(6611771283741804070)
XLA Ops:
  1.8 1.9 %convolution_convert_fusion.4.q_ref = bf16[512,256]{1,0:T(8,128)(2,1)} fusion(bf16[256,256]{1,0:T(8,128)(2,1)S(1)} %copy-done, bf16[1,512,256]{2,1,0:T(8,128)(2,1)} %param.10), kind=kOutput, calls=%fused_computation.17 | convolution fusion | flops 67239936 | bytes 655360 | tf_op jit(solution)/shard_map/dot_general | solution.py:24
  3.7 1.9 %convolution_convert_fusion.3.qt_ref = bf16[256,512]{1,0:T(8,128)(2,1)} fusion(bf16[256,256]{1,0:T(8,128)(2,1)S(1)} %copy-done, bf16[1,512,256]{2,1,0:T(8,128)(2,1)} %param.10), kind=kOutput, calls=%fused_computation.16 | convolution fusion | flops 67239936 | bytes 655360 | tf_op jit(solution)/shard_map/dot_general | solution.py:24
  7.6 0.9 select_reduce_fusion.6
  8.6 20.1 %fetch.1 = (bf16[6,512,256]{2,1,0:T(8,128)(2,1)}, bf16[6,128,256]{2,1,0:T(8,128)(2,1)}, bf16[64,256]{1,0:T(8,128)(2,1)}) custom-call(bf16[512,256]{1,0:T(8,128)(2,1)} %bitcast.147, bf16[512,256]{1,0:T(8,128)(2,1)} %bitcast.146), custom_call_target="tpu_custom_call" | custom-call | tf_op jit(solution)/shard_map/fetch/pallas_call | solution.py:270
  28.8 1.0 slice_bitcast_fusion.11
  29.8 0.8 broadcast_select_fusion.4
  31.7 0.8 copy-done.7
  32.7 0.8 copy.19.do_ref
  36.0 0.8 abs_compare_fusion
  36.8 0.7 and_select_fusion.bias_ref
  37.5 0.9 copy-done.1
  38.4 0.9 copy-done.2
  39.4 0.9 copy-done.3
  40.3 25.1 %attention.1 = (bf16[256,512]{1,0:T(8,128)(2,1)S(1)}, f32[256,512]{1,0:T(8,128)S(1)}, f32[2,768,256]{2,1,0:T(8,128)}, f32[2,768,256]{2,1,0:T(8,128)}) custom-call(f32[2,8,256]{2,1,0:T(8,128)S(1)} %and_select_fusion.bias_ref, bf16[512,256]{1,0:T(8,128)(2,1)S(1)} %copy-done.1, bf16[256,512]{1,0:T(8,128)(2,1)S(1)} %copy-done.2, bf16[512,256]{1,0:T(8,128)(2,1)S(1)} %copy-done.3, ...), custom_call_target="tpu_custom_call" | custom-call | flops 20000000000 | bytes 8000000 | tf_op jit(solution)/shard_map/attention/pallas_call | solution.py:123
  65.4 1.9 %fusion.9 = f32[2,768,256]{2,1,0:T(8,128)S(1)} fusion(f32[2,768,256]{2,1,0:T(8,128)} %get-tuple-element.19, bf16[256,256]{1,0:T(8,128)(2,1)S(1)} %copy-done), kind=kOutput, calls=%fused_computation.43 | convolution fusion | flops 201719808 | bytes 3276800 | tf_op jit(solution)/shard_map/dot_general | solution.py:24
  70.4 1.1 convolution_add_fusion.1.base_ref
  73.6 1.3 %pad_maximum_fusion = f32[1536,256]{1,0:T(8,128)} fusion(f32[768,256]{1,0:T(8,128)S(1)} %bitcast.153, f32[256,256]{1,0:T(8,128)S(1)} %fusion.31, f32[256,256]{1,0:T(8,128)S(1)} %convolution_bitcast_fusion.4, f32[256,256]{1,0:T(8,128)S(1)} %fusion.2), kind=kLoop, calls=%fused_computation | loop fusion | flops 1179648 | bytes 3145728 | tf_op jit(solution)/shard_map/concatenate | solution.py:613
  74.9 0.9 fusion.3
  76.6 1.1 copy-done.10
  77.8 35.9 %reduce.1 = (bf16[512,256]{1,0:T(8,128)(2,1)}, bf16[2,8,96,256]{3,2,1,0:T(8,128)(2,1)}) custom-call(bf16[6,512,256]{2,1,0:T(8,128)(2,1)} %copy-done.10, f32[512,256]{1,0:T(8,128)} %convolution_add_fusion.1.base_ref, f32[2,8,96,256]{3,2,1,0:T(8,128)} %bitcast.148), custom_call_target="tpu_custom_call" | custom-call | tf_op jit(solution)/shard_map/reduce/pallas_call | solution.py:466
  113.7 1.3 %convert_multiply_fusion = f32[2,8,96,256]{3,2,1,0:T(8,128)S(1)} fusion(bf16[2,8,96,256]{3,2,1,0:T(8,128)(2,1)} %get-tuple-element.23), kind=kLoop, calls=%fused_computation.1 | loop fusion | flops 786432 | bytes 2359296 | tf_op jit(solution)/shard_map/mul | solution.py:619
  115.0 0.9 slice.143
  115.9 0.9 fusion.48
  116.8 0.7 copy.37
  (110 shorter events, 11.0 us)
Async XLA Ops:
  0.6 1.2 copy-start
  0.6 7.9 %copy-start.4 = (bf16[1,512,256]{2,1,0:T(8,128)(2,1)S(1)}, bf16[1,512,256]{2,1,0:T(8,128)(2,1)}, u32[]{:S(2)}) copy-start(bf16[1,512,256]{2,1,0:T(8,128)(2,1)} %param.19) | copy-start | bytes 786436
  1.8 28.8 %copy-start.33 = (s32[1,2]{1,0:T(1,128)S(1)}, s32[1,2]{1,0:T(1,128)}, u32[]{:S(2)}) copy-start(s32[1,2]{1,0:T(1,128)} %param.11) | copy-start | bytes 28
  5.6 25.2 %copy-start.5 = (bf16[1,512,256]{2,1,0:T(8,128)(2,1)S(1)}, bf16[1,512,256]{2,1,0:T(8,128)(2,1)}, u32[]{:S(2)}) copy-start(bf16[1,512,256]{2,1,0:T(8,128)(2,1)} %param.19) | copy-start | bytes 786436
  5.6 25.2 %copy-start.14 = (bf16[3,256,256]{2,1,0:T(8,128)(2,1)S(1)}, bf16[3,256,256]{2,1,0:T(8,128)(2,1)}, u32[]{:S(2)}) copy-start(bf16[3,256,256]{2,1,0:T(8,128)(2,1)} %param.18) | copy-start | bytes 1179652
  30.6 3.1 %copy-start.27 = (pred[2]{0:T(512)(128)(4,1)}, pred[2]{0:T(512)(128)(4,1)S(1)}, u32[]{:S(2)}) copy-start(pred[2]{0:T(512)(128)(4,1)S(1)} %get-tuple-element.58) | copy-start | bytes 10
  30.6 3.1 %copy-start.29 = (pred[2]{0:T(512)(128)(4,1)}, pred[2]{0:T(512)(128)(4,1)S(1)}, u32[]{:S(2)}) copy-start(pred[2]{0:T(512)(128)(4,1)S(1)} %get-tuple-element.59) | copy-start | bytes 10
  30.6 3.1 %copy-start.31 = (pred[2]{0:T(512)(128)(4,1)}, pred[2]{0:T(512)(128)(4,1)S(1)}, u32[]{:S(2)}) copy-start(pred[2]{0:T(512)(128)(4,1)S(1)} %get-tuple-element.60) | copy-start | bytes 10
  30.8 3.7 %copy-start.25 = (bf16[2,128,256]{2,1,0:T(8,128)(2,1)}, bf16[2,128,256]{2,1,0:T(8,128)(2,1)S(1)}, u32[]{:S(2)}) copy-start(bf16[2,128,256]{2,1,0:T(8,128)(2,1)S(1)} %get-tuple-element.30) | copy-start | bytes 393220
  30.8 3.6 %copy-start.23 = (bf16[2,128,256]{2,1,0:T(8,128)(2,1)}, bf16[2,128,256]{2,1,0:T(8,128)(2,1)S(1)}, u32[]{:S(2)}) copy-start(bf16[2,128,256]{2,1,0:T(8,128)(2,1)S(1)} %broadcast_select_fusion) | copy-start | bytes 393220
  31.1 1.4 %copy-start.18 = (bf16[256,256]{1,0:T(8,128)(2,1)S(1)}, bf16[256,256]{1,0:T(8,128)(2,1)}, u32[]{:S(2)}) copy-start(bf16[256,256]{1,0:T(8,128)(2,1)} %param.17) | copy-start | bytes 393220
  31.4 2.2 %copy-start.11 = (bf16[6,512,256]{2,1,0:T(8,128)(2,1)S(1)}, bf16[6,512,256]{2,1,0:T(8,128)(2,1)}, u32[]{:S(2)}) copy-start(bf16[6,512,256]{2,1,0:T(8,128)(2,1)} %get-tuple-element.17) | copy-start | bytes 4718596
  65.4 1.9 %copy-start.13 = (f32[2,768,256]{2,1,0:T(8,128)S(1)}, f32[2,768,256]{2,1,0:T(8,128)}, u32[]{:S(2)}) copy-start(f32[2,768,256]{2,1,0:T(8,128)} %get-tuple-element.20) | copy-start | bytes 4718596
  65.4 1.9 %copy-start.22 = (bf16[256,256]{1,0:T(8,128)(2,1)S(1)}, bf16[256,256]{1,0:T(8,128)(2,1)}, u32[]{:S(2)}) copy-start(bf16[256,256]{1,0:T(8,128)(2,1)} %param.16) | copy-start | bytes 393220
  67.8 1.3 %copy-start.8 = (f32[512,256]{1,0:T(8,128)S(1)}, f32[512,256]{1,0:T(8,128)}, u32[]{:S(2)}) copy-start(f32[512,256]{1,0:T(8,128)} %copy-done.7) | copy-start | bytes 1572868
  67.8 1.6 %copy-start.12 = (f32[2,768,256]{2,1,0:T(8,128)S(1)}, f32[2,768,256]{2,1,0:T(8,128)}, u32[]{:S(2)}) copy-start(f32[2,768,256]{2,1,0:T(8,128)} %get-tuple-element.19) | copy-start | bytes 4718596
  67.8 1.7 %copy-start.17 = (bf16[2,512,256]{2,1,0:T(8,128)(2,1)S(1)}, bf16[2,512,256]{2,1,0:T(8,128)(2,1)}, u32[]{:S(2)}) copy-start(bf16[2,512,256]{2,1,0:T(8,128)(2,1)} %copy-done.16) | copy-start | bytes 1572868
  67.9 1.7 %copy-start.24 = (bf16[2,128,256]{2,1,0:T(8,128)(2,1)S(1)}, bf16[2,128,256]{2,1,0:T(8,128)(2,1)}, u32[]{:S(2)}) copy-start(bf16[2,128,256]{2,1,0:T(8,128)(2,1)} %copy-done.23) | copy-start | bytes 393220
  67.9 1.7 %copy-start.26 = (bf16[2,128,256]{2,1,0:T(8,128)(2,1)S(1)}, bf16[2,128,256]{2,1,0:T(8,128)(2,1)}, u32[]{:S(2)}) copy-start(bf16[2,128,256]{2,1,0:T(8,128)(2,1)} %copy-done.25) | copy-start | bytes 393220
  67.9 7.9 %collective-permute-start.1 = (bf16[2,2,64,256]{3,2,1,0:T(8,128)(2,1)S(1)}, bf16[2,2,64,256]{3,2,1,0:T(8,128)(2,1)S(1)}, u32[]{:S(2)}, u32[]{:S(2)}) collective-permute-start(bf16[2,2,64,256]{3,2,1,0:T(8,128)(2,1)S(1)} %fusion.12), channel_id=1, source_target_pairs={{0,1},{1,0},{2,3},{3,2},{4,5},{5,4},{6,7},{7,6},{8,9},{9,8},{10,11... | collective-permute-start | bytes 393224 | tf_op jit(solution)/shard_map/ppermute | solution.py:490
  68.7 3.4 %collective-permute-start = (bf16[1,64,256]{2,1,0:T(8,128)(2,1)S(1)}, bf16[1,64,256]{2,1,0:T(8,128)(2,1)S(1)}, u32[]{:S(2)}, u32[]{:S(2)}) collective-permute-start(bf16[1,64,256]{2,1,0:T(8,128)(2,1)S(1)} %fusion.40), channel_id=1, source_target_pairs={{0,1},{1,0},{2,3},{3,2},{4,5},{5,4},{6,7},{7,6},{8,9},{9,8},{10,11... | collective-permute-start | bytes 98312 | tf_op jit(solution)/shard_map/ppermute | solution.py:490
  70.4 1.4 %copy-start.6 = (bf16[1,512,256]{2,1,0:T(8,128)(2,1)S(1)}, bf16[1,512,256]{2,1,0:T(8,128)(2,1)}, u32[]{:S(2)}) copy-start(bf16[1,512,256]{2,1,0:T(8,128)(2,1)} %param.19) | copy-start | bytes 786436
  76.6 1.1 copy-start.10
  115.0 1.8 %copy-start.20 = (bf16[512,256]{1,0:T(8,128)(2,1)S(1)}, bf16[512,256]{1,0:T(8,128)(2,1)}, u32[]{:S(2)}) copy-start(bf16[512,256]{1,0:T(8,128)(2,1)} %get-tuple-element.22) | copy-start | bytes 786436
  (12 other events, 11.5 us)

commit v3 on v2

--- a/solution.py
+++ b/solution.py
@@ -25,8 +25,10 @@
 
 
 def attention_kernel(
-    bias_ref, q_ref, qt_ref, do_ref, dot_ref, k_ref, v_ref, kt_ref, vt_ref,
-    mixt_ref, dqt_ref, dk_ref, dv_ref,
+    meta_ref, buf_ref, halo_ref, x_ref, q_ref, qt_ref, do_ref, dot_ref, resid_ref,
+    sp_ref, vp_ref, op_ref,
+    residual_ref, hidden_ref, base_ref, part_ref, gs_ref, gv_ref, go_ref,
+    xs_ref, k_ref, v_ref, kt_ref, vt_ref, mixt_ref, dqt_ref, dk_ref, dv_ref,
     s_scr, dp_scr, p_scr, ds_scr, qm_scr, dom_scr,
 ):
     tokens, width = q_ref.shape
@@ -41,6 +43,39 @@
 
     dk_ref[...] = jnp.zeros_like(dk_ref)
     dv_ref[...] = jnp.zeros_like(dv_ref)
+    rim = WMAX * COLS
+    window = meta_ref[2]
+    row_id = meta_ref[3]
+    first_row = row_id * (tokens // COLS)
+    total_rows = meta_ref[4]
+    zero_rim = jnp.zeros((rim, width), BF)
+    for s in range(2):
+        kind = meta_ref[s]
+        xs_ref[s, rim : rim + tokens, :] = buf_ref[kind]
+
+        @pl.when(row_id == 0)
+        def _():
+            xs_ref[s, :rim, :] = zero_rim
+            xs_ref[s, rim + tokens :, :] = halo_ref[kind]
+
+        @pl.when(row_id != 0)
+        def _():
+            xs_ref[s, :rim, :] = halo_ref[kind]
+            xs_ref[s, rim + tokens :, :] = zero_rim
+
+        xs = xs_ref[s]
+        keys = mm(xs, sp_ref[...]).astype(BF)
+        vals = mm(xs, vp_ref[...]).astype(BF)
+        k_ref[s] = keys
+        v_ref[s] = vals
+        kt_ref[s] = keys.T
+        vt_ref[s] = vals.T
+    query_row = lax.broadcasted_iota(jnp.int32, (1, nq), 1) // COLS
+
+    def bias_row(b, c):
+        key_row = first_row + b * QBLK + c - WMAX
+        reach = jnp.where((key_row >= 0) & (key_row < total_rows), window, -1)
+        return jnp.where(jnp.abs(c - WMAX - query_row) <= reach, 0.0, -jnp.inf).astype(F32)
 
     for b in range(blocks):
         q0 = b * nq
@@ -70,14 +105,14 @@
                 m8 = jnp.full((8, nq), -jnp.inf, F32)
                 for c in range(2 * rows):
                     x = s_scr[c * COLS : (c + 1) * COLS, :].reshape(COLS // 8, 8, nq)
-                    m8 = jnp.maximum(m8, jnp.max(x, axis=0) + bias_ref[b, c % rows, :][None, :])
+                    m8 = jnp.maximum(m8, jnp.max(x, axis=0) + bias_row(b, c % rows))
                 m = jnp.max(m8, axis=0, keepdims=True)
                 kk = SCORE_SCALE * LOG2E
                 l8 = jnp.zeros((8, nq), F32)
                 u8 = jnp.zeros((8, nq), F32)
                 for c in range(2 * rows):
                     sl = slice(c * COLS, (c + 1) * COLS)
-                    off = (bias_ref[b, c % rows, :][None, :] - m) * kk
+                    off = (bias_row(b, c % rows) - m) * kk
                     p = jnp.exp2(s_scr[sl, :] * kk + off)
                     s_scr[sl, :] = p
                     l8 = l8 + jnp.sum(p.reshape(COLS // 8, 8, nq), axis=0)
@@ -113,24 +148,55 @@
             dk_ref[s, q0 : q0 + span, :] += mm(ds_scr[ks, :], qm_scr[...])
             dv_ref[s, q0 : q0 + span, :] += mm(p_scr[ks, :], dom_scr[...])
 
-
-def attention(bias, q, qt, do, dot, k, v, kt, vt):
+    dq = dqt_ref[...].T.astype(BF)
+    base_ref[...] = resid_ref[...] + mm(dq, sp_ref[...], 1, 1)
+    mixt = mixt_ref[...]
+    go_ref[...] = mm(mixt, resid_ref[...].astype(BF))
+    residual = x_ref[...].astype(F32) + mm(mixt.T, op_ref[...])
+    residual_ref[...] = residual
+    hidden_ref[...] = residual.astype(BF)
+    gs = mm(x_ref[...].T, dq)
+    gv = jnp.zeros((width, width), F32)
+    for s in range(2):
+        dk = dk_ref[s].astype(BF)
+        dv = dv_ref[s].astype(BF)
+        part_ref[s] = mm(dk, sp_ref[...], 1, 1) + mm(dv, vp_ref[...], 1, 1)
+        xst = xs_ref[s].T
+        gs = gs + mm(xst, dk)
+        gv = gv + mm(xst, dv)
+    gs_ref[...] = gs
+    gv_ref[...] = gv
+
+
+def attention(meta, buf, halo, x, q, qt, do, dot, resid, shared, value, output):
     tokens, width = q.shape
-    ext = k.shape[1]
+    ext = tokens + 2 * WMAX * COLS
     nq = QBLK * COLS
     keys = 2 * (QBLK + 2 * WMAX) * COLS
     vm = pl.BlockSpec(memory_space=pltpu.VMEM)
+    full = jax.ShapeDtypeStruct((tokens, width), F32)
+    square = jax.ShapeDtypeStruct((width, width), F32)
     return pl.pallas_call(
         attention_kernel,
         out_shape=(
-            jax.ShapeDtypeStruct((width, tokens), BF),
-            jax.ShapeDtypeStruct((width, tokens), F32),
+            full,
+            jax.ShapeDtypeStruct((tokens, width), BF),
+            full,
             jax.ShapeDtypeStruct((2, ext, width), F32),
-            jax.ShapeDtypeStruct((2, ext, width), F32),
+            square, square, square,
         ),
-        in_specs=[vm] * 9,
-        out_specs=(vm,) * 4,
+        in_specs=[pl.BlockSpec(memory_space=pltpu.SMEM)] + [vm] * 11,
+        out_specs=(vm,) * 7,
         scratch_shapes=[
+            pltpu.VMEM((2, ext, width), BF),
+            pltpu.VMEM((2, ext, width), BF),
+            pltpu.VMEM((2, ext, width), BF),
+            pltpu.VMEM((2, width, ext), BF),
+            pltpu.VMEM((2, width, ext), BF),
+            pltpu.VMEM((width, tokens), BF),
+            pltpu.VMEM((width, tokens), F32),
+            pltpu.VMEM((2, ext, width), F32),
+            pltpu.VMEM((2, ext, width), F32),
             pltpu.VMEM((keys, nq), F32),
             pltpu.VMEM((keys, nq), F32),
             pltpu.VMEM((keys, HEADS * nq), BF),
@@ -143,7 +209,7 @@
             flops=int(2e10), bytes_accessed=int(8e6), transcendentals=int(4e6)
         ),
         name="attention",
-    )(bias, q, qt, do, dot, k, v, kt, vt)
+    )(meta, buf, halo, x, q, qt, do, dot, resid, shared, value, output)
 
 
 MESH = pl.DeviceIdType.MESH
@@ -163,7 +229,11 @@
     pl.semaphore_wait(barrier, count)
 
 
-def fetch_kernel(frames, x_ref, ct_ref, buf_ref, halo_ref, cth_ref, ssem, rsem, hs, hr, cs, cr):
+def fetch_kernel(
+    frames, level_ref, x_ref, ct_ref, qs_ref, sp_ref, op_ref, taps_ref,
+    buf_ref, halo_ref, q_ref, qt_ref, do_ref, dot_ref, gzb_ref, resid_ref, gain_ref,
+    cth_ref, ext_ref, ssem, rsem, hs, hr, cs, cr,
+):
     f = lax.axis_index("frame")
     r = lax.axis_index("row")
     tokens = x_ref.shape[0]
@@ -230,6 +300,40 @@
         def _():
             copy(5, c, buf_ref.at[1], across).start()
 
+    level = lax.broadcasted_iota(jnp.int32, (qs_ref.shape[0], 1), 0)
+    gain = jnp.sum(
+        jnp.where(level == level_ref[0], qs_ref[...], 0.0), axis=0, keepdims=True
+    )
+    gain_ref[...] = gain
+    queries = mm(x_ref[...], sp_ref[...]).astype(BF)
+    q_ref[...] = queries
+    qt_ref[...] = queries.T
+    grad_z = ct_ref[...].astype(F32) * gain
+    grad_zb = grad_z.astype(BF)
+    gzb_ref[...] = grad_zb
+    ct_copy.wait()
+    outer = (cth_ref[...].astype(F32) * gain).astype(BF)
+    blank = jnp.zeros_like(outer)
+    ext_ref[COLS : COLS + tokens, :] = grad_zb
+
+    @pl.when(r == 0)
+    def _():
+        ext_ref[:COLS, :] = blank
+        ext_ref[COLS + tokens :, :] = outer
+
+    @pl.when(r != 0)
+    def _():
+        ext_ref[:COLS, :] = outer
+        ext_ref[COLS + tokens :, :] = blank
+
+    resid = grad_z
+    for t in range(3):
+        resid = resid + mm(ext_ref[(2 - t) * COLS : (2 - t) * COLS + tokens, :], taps_ref[t], 1, 1)
+    resid_ref[...] = resid
+    grad_mixed = mm(resid.astype(BF), op_ref[...], 1, 1).astype(BF)
+    do_ref[...] = grad_mixed
+    dot_ref[...] = grad_mixed.T
+
     rim = WMAX * COLS
     start = pl.multiple_of((1 - r) * (tokens - rim), rim)
 
@@ -260,28 +364,32 @@
             for c in range(CHUNKS):
                 copy(kind, c, x_ref, across).wait_send()
 
-    ct_copy.wait()
-
-
-def fetch(tokens, cotangent, frames):
+
+def fetch(level, tokens, cotangent, scale, shared, output, taps, frames):
     count, width = tokens.shape
     vm = pl.BlockSpec(memory_space=pltpu.VMEM)
     dma = pltpu.SemaphoreType.DMA
+    rows = jax.ShapeDtypeStruct((count, width), BF)
+    columns = jax.ShapeDtypeStruct((width, count), BF)
     return pl.pallas_call(
         functools.partial(fetch_kernel, frames),
         out_shape=(
             jax.ShapeDtypeStruct((6, count, width), BF),
             jax.ShapeDtypeStruct((6, WMAX * COLS, width), BF),
-            jax.ShapeDtypeStruct((COLS, width), BF),
+            rows, columns, rows, columns, rows,
+            jax.ShapeDtypeStruct((count, width), F32),
+            jax.ShapeDtypeStruct((1, width), F32),
         ),
-        in_specs=[vm] * 2,
-        out_specs=(vm,) * 3,
+        in_specs=[pl.BlockSpec(memory_space=pltpu.SMEM)] + [vm] * 6,
+        out_specs=(vm,) * 9,
         scratch_shapes=[
+            pltpu.VMEM((COLS, width), BF),
+            pltpu.VMEM((count + 2 * COLS, width), BF),
             dma((6, CHUNKS)), dma((6, CHUNKS)), dma((6,)), dma((6,)), dma(()), dma(()),
         ],
         compiler_params=pltpu.CompilerParams(collective_id=0, has_side_effects=True),
         name="fetch",
-    )(tokens, cotangent)
+    )(level, tokens, cotangent, scale, shared, output, taps)
 
 
 def reduce_kernel(
@@ -512,7 +620,6 @@
     frame_id = lax.axis_index("frame")
     row_id = lax.axis_index("row")
     own_refs = ref_frames[0]
-    window = windows[0]
     ext_rows = rows_dev + 2 * WMAX
     grid = (rows_dev, COLS, width)
     tokens = latents[0]
@@ -522,65 +629,24 @@
         frame_id - 2, frame_id + 2, frame_id + 1 - 2 * odd,
         frame_id - 4, frame_id + 4, frame_id - 1 + 2 * odd,
     )
-    buf, halo, ct_edge = fetch(tokens, cotangent[0], frames)
-    slot = jnp.zeros((2,) + tokens.shape, BF)
-    rim = jnp.zeros((2, WMAX * COLS, width), BF)
+    buf, halo, q, qt, do, dot, grad_zb, grad_resid, gain = fetch(
+        quant_level, tokens, cotangent[0], quant_scale, shared_proj, output_proj, conv_taps, frames
+    )
+    kinds = jnp.zeros((2,), jnp.int32)
     for kind, source in enumerate(sources):
-        matched = (own_refs == source).reshape(2, 1, 1)
-        slot = jnp.where(matched, buf[kind][None], slot)
-        rim = jnp.where(matched, halo[kind][None], rim)
-    zero = jnp.zeros_like(rim)
-    slot_ext = jnp.concatenate(
-        [jnp.where(row_id == 0, zero, rim), slot, jnp.where(row_id == 0, rim, zero)], axis=1
-    )
-    slot_flat = slot_ext.reshape(2, ext_rows * COLS, width)
-    q = mm(tokens, shared_proj).astype(BF)
-    qt = mm(shared_proj, tokens, 0, 1).astype(BF)
-    k = mm(slot_flat, shared_proj, 2, 0).astype(BF)
-    v = mm(slot_flat, value_proj, 2, 0).astype(BF)
-    kt = jnp.transpose(k, (0, 2, 1))
-    vt = jnp.transpose(v, (0, 2, 1))
-
-    levels = jnp.arange(quant_scale.shape[0], dtype=jnp.int32)
-    gain = jnp.sum(jnp.where((levels == quant_level[0])[:, None], quant_scale, 0.0), axis=0)[None]
-    grad_z = cotangent[0].astype(F32) * gain
-    grad_zb = grad_z.astype(BF)
-    edge = (ct_edge.astype(F32) * gain).astype(BF)
-    blank = jnp.zeros_like(edge)
-    grad_ext = jnp.concatenate(
-        [jnp.where(row_id == 0, blank, edge), grad_zb, jnp.where(row_id == 0, edge, blank)], axis=0
-    )
-    grad_resid = grad_z
-    for t in range(3):
-        part = grad_ext[(2 - t) * COLS : (2 - t + rows_dev) * COLS]
-        grad_resid = grad_resid + mm(part, conv_taps[t], 1, 1)
-    grad_rb = grad_resid.astype(BF)
-    do = mm(grad_rb, output_proj, 1, 1).astype(BF)
-    dot = jnp.transpose(do)
-
-    blocks = rows_dev // QBLK
-    span_rows = QBLK + 2 * WMAX
-    b_i = jnp.arange(blocks, dtype=jnp.int32)[:, None, None]
-    r_i = jnp.arange(span_rows, dtype=jnp.int32)[None, :, None]
-    i_i = (jnp.arange(QBLK * COLS, dtype=jnp.int32) // COLS)[None, None, :]
-    key_row = row_id * rows_dev + b_i * QBLK + r_i - WMAX
-    allowed = (jnp.abs(r_i - WMAX - i_i) <= window) & (key_row >= 0) & (key_row < total_rows)
-    bias = jnp.where(allowed, 0.0, -jnp.inf).astype(F32)
-
-    mixt, dqt, dk, dv = attention(bias, q, qt, do, dot, k, v, kt, vt)
-
-    residual = tokens.astype(F32) + mm(mixt, output_proj, 0, 0)
-    hidden_ext = row_halo(residual.astype(BF).reshape(grid), row_id, 1).reshape(-1, width)
+        kinds = jnp.where(own_refs == source, kind, kinds)
+    rest = jnp.stack([windows[0], row_id, jnp.int32(total_rows)]).astype(jnp.int32)
+    meta = jnp.concatenate([kinds, rest])
+    residual, hidden, grad_latents, partial, grad_shared, grad_values, grad_output = attention(
+        meta, buf, halo, tokens, q, qt, do, dot, grad_resid, shared_proj, value_proj, output_proj
+    )
+    hidden_ext = row_halo(hidden.reshape(grid), row_id, 1).reshape(-1, width)
     context = residual
     for t in range(3):
         context = context + mm(hidden_ext[t * COLS : (t + rows_dev) * COLS], conv_taps[t])
     coded = (context * gain).astype(BF)
 
-    dkb = dk.astype(BF)
-    dvb = dv.astype(BF)
-    partial = (mm(dkb, shared_proj, 2, 1) + mm(dvb, value_proj, 2, 1)).reshape(
-        2, ext_rows, COLS, width
-    )
+    partial = partial.reshape(2, ext_rows, COLS, width)
     upper = partial[:, :WMAX]
     lower = partial[:, WMAX + rows_dev :]
     got = from_partner(jnp.where(row_id == 0, lower, upper).astype(BF)).astype(F32)
@@ -590,7 +656,6 @@
         + jnp.concatenate([jnp.where(row_id == 0, 0.0, got), filler], axis=1)
         + jnp.concatenate([filler, jnp.where(row_id == 0, got, 0.0)], axis=1)
     )
-    grad_latents = grad_resid + mm(dqt.astype(BF), shared_proj, 0, 1)
     targets = (
         frame_id + 2, frame_id - 2, frame_id + 1 - 2 * odd,
         frame_id + 4, frame_id - 4, frame_id - 1 + 2 * odd,
@@ -603,10 +668,6 @@
             for t in targets
         ]
     )
-    flat = slot_flat.reshape(-1, width)
-    grad_shared = mm(tokens, dqt.astype(BF), 0, 1) + mm(flat, dkb.reshape(-1, width), 0, 0)
-    grad_values = mm(flat, dvb.reshape(-1, width), 0, 0)
-    grad_output = mm(mixt, grad_rb)
     grad_taps = jnp.stack(
         [mm(hidden_ext[t * COLS : (t + rows_dev) * COLS], grad_zb, 0, 0) for t in range(3)]
     )

time: 118 us -> 110 us (0.932)
  matrix products: 12.8 us -> 2.19 us
  other arithmetic: 8.71 us -> 5.06 us
  local copies, waits for them, and re-layouts: 11.3 us -> 14.6 us
  Pallas kernels: 81.2 us -> 84.4 us
    dot_general x22 -> x6, matrix products: 12.8 us -> 2.19 us  [mm(): lax.dot_general(a, b, (((ca,), (cb,)), ((), ())), preferred_element_type=...]
    unnamed x74 -> x42, local copies, waits for them, and re-layouts: 6.95 us -> 12.8 us
    pallas_call x1, Pallas kernels: 25.1 us -> 27.6 us  [attention(): pl.pallas_call(attention_kernel, out_shape=(full, jax.ShapeDtypeStruct((t...]
    select_n x6 -> x1, other arithmetic: 2.48 us -> 0.67 us  [local(): kinds = jnp.where(own_refs == source, kind, kinds)]
    convert_element_type x3 -> x0, local copies, waits for them, and re-layouts: 1.38 us -> none  [the longest x1 0.84 us: local(): do = mm(grad_rb, output_proj, 1, 1).astype(BF)]
  transfers between devices with their start and end apart: 2 -> 2, of which waited for: 0 -> 0; matrix products, arithmetic and copies ran while one was open for 5% -> 4% of each run, Pallas kernels for 0% -> 0%
where the time goes in v3:
time: 110 us; the launch traced here: 109 us
  Pallas kernels  84.4 us (77%)
  local copies, waits for them, and re-layouts  14.6 us (13%)
  other arithmetic  5.06 us (5%)
  matrix products  2.19 us (2%)
  between operations  2.17 us (2%)
    pallas_call x1, Pallas kernels, reduce(): pl.pallas_call(functools.partial(reduce_kernel, frames), out_shape=(jax.S...  35.9 us
    pallas_call x1, Pallas kernels, attention(): pl.pallas_call(attention_kernel, out_shape=(full, jax.ShapeDtypeStruct((t...  27.6 us
    pallas_call x1, Pallas kernels, fetch(): pl.pallas_call(functools.partial(fetch_kernel, frames), out_shape=(jax.Sh...  20.8 us
    unnamed x42, local copies, waits for them, and re-layouts  12.8 us
  transfers between devices with their start and end apart: 2, of which 0 were waited for; matrix products, arithmetic and copies ran while one was open for 4% of the time, Pallas kernels for 0%

profile of v3, /device:TPU:0, one launch (start us, length us, event | category | flops | bytes accessed | tf_op | source)
XLA Modules:
  0.0 109.1 jit_solution(2657346252323531191)
XLA Ops:
  1.9 0.7 select_select_fusion
  2.7 20.8 %fetch.1 = (bf16[6,512,256]{2,1,0:T(8,128)(2,1)}, bf16[6,128,256]{2,1,0:T(8,128)(2,1)}, bf16[512,256]{1,0:T(8,128)(2,1)}, bf16[256,512]{1,0:T(8,128)(2,1)}, bf16...) custom-call(s32[1]{0:T(128)S(6)} %copy.23.level_ref, ...), custom_call_target="tpu_custom_call" | custom-call | tf_op jit(solution)/shard_map/fetch/pallas_call | solution.py:374
  23.5 0.9 copy-done.1
  24.5 0.9 copy-done.2
  25.4 0.9 copy-done.3
  26.3 1.0 copy-done.4
  27.3 1.0 copy-done.5
  28.3 0.9 copy-done.6
  29.3 0.9 copy-done.7
  30.2 0.9 copy-done.8
  31.2 0.9 copy-done.9
  32.1 0.9 copy-done.10
  33.0 27.6 %attention.1 = (f32[512,256]{1,0:T(8,128)S(1)}, bf16[512,256]{1,0:T(8,128)(2,1)S(1)}, f32[512,256]{1,0:T(8,128)S(1)}, f32[2,768,256]{2,1,0:T(8,128)}, f32[256,25...) custom-call(s32[5]{0:T(128)S(1)} %pad_add_fusion.meta_ref, ...), custom_call_target="tpu_custom_call" | custom-call | flops 20000000000 | bytes 8000000 | tf_op jit(solution)/shard_map/attention/pallas_call | solution.py:179
  60.7 0.8 copy-done
  61.9 1.1 fusion.4
  64.7 1.3 %pad_maximum_fusion = f32[1536,256]{1,0:T(8,128)} fusion(f32[768,256]{1,0:T(8,128)S(1)} %bitcast.81, f32[256,256]{1,0:T(8,128)S(1)} %get-tuple-element.38, f32[256,256]{1,0:T(8,128)S(1)} %get-tuple-element.37, f32[256,256]{1,0:T(8,128)S(1)} %get-tuple-element.36), kind=kLoop, calls=%fused_computation | loop fusion | flops 1179648 | bytes 3145728 | tf_op jit(solution)/shard_map/concatenate | solution.py:674
  65.9 0.9 fusion.2
  67.4 0.5 select_reduce_fusion
  68.1 1.1 %copy-done.12 = bf16[6,512,256]{2,1,0:T(8,128)(2,1)} copy-done((bf16[6,512,256]{2,1,0:T(8,128)(2,1)}, bf16[6,512,256]{2,1,0:T(8,128)(2,1)S(1)}, u32[]{:S(2)}) %copy-start.12) | copy-done | bytes 1572888
  69.3 35.9 %reduce.1 = (bf16[512,256]{1,0:T(8,128)(2,1)}, bf16[2,8,96,256]{3,2,1,0:T(8,128)(2,1)}) custom-call(bf16[6,512,256]{2,1,0:T(8,128)(2,1)} %copy-done.12, f32[512,256]{1,0:T(8,128)} %copy-done, f32[2,8,96,256]{3,2,1,0:T(8,128)} %bitcast.79), custom_call_target="tpu_custom_call" | custom-call | tf_op jit(solution)/shard_map/reduce/pallas_call | solution.py:574
  105.2 1.3 %convert_multiply_fusion = f32[2,8,96,256]{3,2,1,0:T(8,128)S(1)} fusion(bf16[2,8,96,256]{3,2,1,0:T(8,128)(2,1)} %get-tuple-element.41), kind=kLoop, calls=%fused_computation.1 | loop fusion | flops 786432 | bytes 2359296 | tf_op jit(solution)/shard_map/mul | solution.py:680
  106.5 0.9 slice.80
  107.5 0.9 fusion.11
  108.4 0.7 copy.24
  (46 shorter events, 2.8 us)
Async XLA Ops:
  23.5 1.0 copy-start.1
  24.5 0.9 copy-start.2
  25.4 0.9 copy-start.3
  26.3 1.0 copy-start.4
  27.3 1.0 copy-start.5
  28.3 0.9 copy-start.6
  29.3 0.9 copy-start.7
  30.2 0.9 copy-start.8
  31.2 0.9 copy-start.9
  32.1 0.9 copy-start.10
  33.0 30.2 %copy-start.17 = (s32[1,2]{1,0:T(1,128)S(1)}, s32[1,2]{1,0:T(1,128)}, u32[]{:S(2)}) copy-start(s32[1,2]{1,0:T(1,128)} %param.11) | copy-start | bytes 28
  33.0 30.2 %copy-start.11 = (bf16[512,256]{1,0:T(8,128)(2,1)S(1)}, bf16[512,256]{1,0:T(8,128)(2,1)}, u32[]{:S(2)}) copy-start(bf16[512,256]{1,0:T(8,128)(2,1)} %get-tuple-element.39) | copy-start | bytes 786436
  60.7 0.8 copy-start
  61.5 2.3 %copy-start.13 = (bf16[3,256,256]{2,1,0:T(8,128)(2,1)S(1)}, bf16[3,256,256]{2,1,0:T(8,128)(2,1)}, u32[]{:S(2)}) copy-start(bf16[3,256,256]{2,1,0:T(8,128)(2,1)} %taps_ref.1) | copy-start | bytes 1179652
  61.5 2.0 %collective-permute-start = (bf16[1,64,256]{2,1,0:T(8,128)(2,1)S(1)}, bf16[1,64,256]{2,1,0:T(8,128)(2,1)S(1)}, u32[]{:S(2)}, u32[]{:S(2)}) collective-permute-start(bf16[1,64,256]{2,1,0:T(8,128)(2,1)S(1)} %select_bitcast_fusion), channel_id=1, source_target_pairs={{0,1},{1,0},{2,3},{3,2},{4,5},{5,4},{6,7},{7,6},{8,9},{9,8},{10,11... | collective-permute-start | bytes 98312 | tf_op jit(solution)/shard_map/ppermute | solution.py:598
  63.0 3.9 %collective-permute-start.1 = (bf16[2,2,64,256]{3,2,1,0:T(8,128)(2,1)S(1)}, bf16[2,2,64,256]{3,2,1,0:T(8,128)(2,1)S(1)}, u32[]{:S(2)}, u32[]{:S(2)}) collective-permute-start(bf16[2,2,64,256]{3,2,1,0:T(8,128)(2,1)S(1)} %fusion.4), channel_id=1, source_target_pairs={{0,1},{1,0},{2,3},{3,2},{4,5},{5,4},{6,7},{7,6},{8,9},{9,8},{10,11... | collective-permute-start | bytes 393224 | tf_op jit(solution)/shard_map/ppermute | solution.py:598
  64.6 1.3 %copy-start.16 = (f32[1,256]{1,0:T(1,128)S(1)}, f32[1,256]{1,0:T(1,128)}, u32[]{:S(2)}) copy-start(f32[1,256]{1,0:T(1,128)} %get-tuple-element.33) | copy-start | bytes 3076
  65.9 1.5 %copy-start.14 = (f32[2,768,256]{2,1,0:T(8,128)S(1)}, f32[2,768,256]{2,1,0:T(8,128)}, u32[]{:S(2)}) copy-start(f32[2,768,256]{2,1,0:T(8,128)} %get-tuple-element.34) | copy-start | bytes 4718596
  68.1 1.2 %copy-start.12 = (bf16[6,512,256]{2,1,0:T(8,128)(2,1)}, bf16[6,512,256]{2,1,0:T(8,128)(2,1)S(1)}, u32[]{:S(2)}) copy-start(bf16[6,512,256]{2,1,0:T(8,128)(2,1)S(1)} %bitcast_dynamic-update-slice_fusion.out_ref) | copy-start | bytes 4718596
  106.5 1.8 %copy-start.15 = (bf16[512,256]{1,0:T(8,128)(2,1)S(1)}, bf16[512,256]{1,0:T(8,128)(2,1)}, u32[]{:S(2)}) copy-start(bf16[512,256]{1,0:T(8,128)(2,1)} %get-tuple-element.40) | copy-start | bytes 786436

commit v4 on v3

--- a/solution.py
+++ b/solution.py
@@ -25,11 +25,12 @@
 
 
 def attention_kernel(
-    meta_ref, buf_ref, halo_ref, x_ref, q_ref, qt_ref, do_ref, dot_ref, resid_ref,
+    meta_ref, buf_hbm, halo_hbm, x_hbm, q_hbm, qt_hbm, do_hbm, dot_hbm, resid_hbm,
     sp_ref, vp_ref, op_ref,
     residual_ref, hidden_ref, base_ref, part_ref, gs_ref, gv_ref, go_ref,
     xs_ref, k_ref, v_ref, kt_ref, vt_ref, mixt_ref, dqt_ref, dk_ref, dv_ref,
     s_scr, dp_scr, p_scr, ds_scr, qm_scr, dom_scr,
+    x_ref, q_ref, qt_ref, do_ref, dot_ref, resid_ref, sems,
 ):
     tokens, width = q_ref.shape
     nq = QBLK * COLS
@@ -48,21 +49,28 @@
     row_id = meta_ref[3]
     first_row = row_id * (tokens // COLS)
     total_rows = meta_ref[4]
-    zero_rim = jnp.zeros((rim, width), BF)
+    bottom = rim + tokens
+    held = pl.multiple_of(jnp.where(row_id == 0, bottom, 0), rim)
+    empty = pl.multiple_of(jnp.where(row_id == 0, 0, bottom), rim)
+    moves = []
     for s in range(2):
         kind = meta_ref[s]
-        xs_ref[s, rim : rim + tokens, :] = buf_ref[kind]
-
-        @pl.when(row_id == 0)
-        def _():
-            xs_ref[s, :rim, :] = zero_rim
-            xs_ref[s, rim + tokens :, :] = halo_ref[kind]
-
-        @pl.when(row_id != 0)
-        def _():
-            xs_ref[s, :rim, :] = halo_ref[kind]
-            xs_ref[s, rim + tokens :, :] = zero_rim
-
+        moves.append((buf_hbm.at[kind], xs_ref.at[s, pl.ds(rim, tokens)]))
+        moves.append((halo_hbm.at[kind], xs_ref.at[s, pl.ds(held, rim)]))
+    moves += [
+        (q_hbm, q_ref), (do_hbm, do_ref), (qt_hbm, qt_ref), (dot_hbm, dot_ref),
+        (x_hbm, x_ref), (resid_hbm, resid_ref),
+    ]
+    copies = [
+        pltpu.make_async_copy(source, target, sems.at[i])
+        for i, (source, target) in enumerate(moves)
+    ]
+    for move in copies:
+        move.start()
+    for s in range(2):
+        xs_ref[s, pl.ds(empty, rim), :] = jnp.zeros((rim, width), BF)
+        copies[2 * s].wait()
+        copies[2 * s + 1].wait()
         xs = xs_ref[s]
         keys = mm(xs, sp_ref[...]).astype(BF)
         vals = mm(xs, vp_ref[...]).astype(BF)
@@ -70,6 +78,8 @@
         v_ref[s] = vals
         kt_ref[s] = keys.T
         vt_ref[s] = vals.T
+    for move in copies[4:]:
+        move.wait()
     query_row = lax.broadcasted_iota(jnp.int32, (1, nq), 1) // COLS
 
     def bias_row(b, c):
@@ -185,7 +195,9 @@
             jax.ShapeDtypeStruct((2, ext, width), F32),
             square, square, square,
         ),
-        in_specs=[pl.BlockSpec(memory_space=pltpu.SMEM)] + [vm] * 11,
+        in_specs=[pl.BlockSpec(memory_space=pltpu.SMEM)]
+        + [pl.BlockSpec(memory_space=pltpu.MemorySpace.HBM)] * 8
+        + [vm] * 3,
         out_specs=(vm,) * 7,
         scratch_shapes=[
             pltpu.VMEM((2, ext, width), BF),
@@ -203,8 +215,15 @@
             pltpu.VMEM((keys, HEADS * nq), BF),
             pltpu.VMEM((HEADS * nq, width), BF),
             pltpu.VMEM((HEADS * nq, width), BF),
+            pltpu.VMEM((tokens, width), BF),
+            pltpu.VMEM((tokens, width), BF),
+            pltpu.VMEM((width, tokens), BF),
+            pltpu.VMEM((tokens, width), BF),
+            pltpu.VMEM((width, tokens), BF),
+            pltpu.VMEM((tokens, width), F32),
+            pltpu.SemaphoreType.DMA((10,)),
         ],
-        compiler_params=pltpu.CompilerParams(vmem_limit_bytes=48 << 20),
+        compiler_params=pltpu.CompilerParams(vmem_limit_bytes=66_000_000),
         cost_estimate=pl.CostEstimate(
             flops=int(2e10), bytes_accessed=int(8e6), transcendentals=int(4e6)
         ),

time: 110 us -> 103 us (0.936)
  local copies, waits for them, and re-layouts: 14.6 us -> 4.36 us
  other arithmetic: 5.06 us -> 7.33 us
    unnamed x42 -> x30, local copies, waits for them, and re-layouts: 12.8 us -> 2.51 us
  transfers between devices with their start and end apart: 2 -> 2, of which waited for: 0 -> 0; matrix products, arithmetic and copies ran while one was open for 4% -> 5% of each run, Pallas kernels for 0% -> 0%
where the time goes in v4:
time: 103 us
  Pallas kernels  85.3 us (83%)
  other arithmetic  7.33 us (7%)
  local copies, waits for them, and re-layouts  4.36 us (4%)
  matrix products  3.14 us (3%)
  between operations  2.23 us (2%)
    pallas_call x1, Pallas kernels, reduce(): pl.pallas_call(functools.partial(reduce_kernel, frames), out_shape=(jax.S...  35.9 us
    pallas_call x1, Pallas kernels, attention(): pl.pallas_call(attention_kernel, out_shape=(full, jax.ShapeDtypeStruct((t...  28.5 us
    pallas_call x1, Pallas kernels, fetch(): pl.pallas_call(functools.partial(fetch_kernel, frames), out_shape=(jax.Sh...  20.9 us
    dot_general x6, matrix products, mm(): lax.dot_general(a, b, (((ca,), (cb,)), ((), ())), preferred_element_type=...  3.14 us
    unnamed x30, local copies, waits for them, and re-layouts  2.51 us
  transfers between devices with their start and end apart: 2, of which 0 were waited for; matrix products, arithmetic and copies ran while one was open for 5% of the time, Pallas kernels for 0%

profile of v4, /device:TPU:0, one launch (start us, length us, event | category | flops | bytes accessed | tf_op | source)
XLA Modules:
  0.0 103.0 jit_solution(12024245787312903546)
XLA Ops:
  1.9 0.7 select_select_fusion
  2.6 0.6 pad_add_fusion.meta_ref
  3.2 20.9 %fetch.1 = (bf16[6,512,256]{2,1,0:T(8,128)(2,1)}, bf16[6,128,256]{2,1,0:T(8,128)(2,1)}, bf16[512,256]{1,0:T(8,128)(2,1)}, bf16[256,512]{1,0:T(8,128)(2,1)}, bf16...) custom-call(s32[1]{0:T(128)S(6)} %copy.23.level_ref, ...), custom_call_target="tpu_custom_call" | custom-call | tf_op jit(solution)/shard_map/fetch/pallas_call | solution.py:393
  24.1 28.5 %attention.1 = (f32[512,256]{1,0:T(8,128)}, bf16[512,256]{1,0:T(8,128)(2,1)}, f32[512,256]{1,0:T(8,128)}, f32[2,768,256]{2,1,0:T(8,128)}, f32[256,256]{1,0:T(8,1...) custom-call(s32[5]{0:T(128)} %pad_add_fusion.meta_ref, bf16[6,512,256]{2,1,0:T(8,128)(2,1)} %get-tuple-element.24.buf_hbm, ...), custom_call_target="tpu_custom_call" | custom-call | flops 20000000000 | bytes 8000000 | tf_op jit(solution)/shard_map/attention/pallas_call | solution.py:189
  52.7 0.9 select_bitcast_fusion
  53.6 0.3 collective-permute-start
  53.9 1.1 %fusion.4 = bf16[2,2,64,256]{3,2,1,0:T(8,128)(2,1)S(1)} fusion(f32[2,12,64,256]{3,2,1,0:T(8,128)} %bitcast.84, pred[]{:T(512)S(6)} %eq.115), kind=kLoop, calls=%fused_computation.23 | loop fusion | flops 65536 | bytes 393217 | tf_op jit(solution)/shard_map/convert_element_type | solution.py:671
  55.0 0.2 collective-permute-start.1
  55.2 1.2 %convolution_bitcast_fusion.1 = f32[1,256,256]{2,1,0:T(8,128)S(1)} fusion(bf16[512,256]{1,0:T(8,128)(2,1)} %get-tuple-element.32, bf16[512,256]{1,0:T(8,128)(2,1)S(1)} %copy-done.1), kind=kOutput, calls=%fused_computation.8 | convolution fusion | flops 67108864 | bytes 786432 | tf_op jit(solution)/shard_map/dot_general | solution.py:24
  56.5 0.3 convolution_bitcast_fusion.2
  56.8 0.2 convolution_add_fusion.2
  57.1 0.2 convolution_add_fusion.1
  57.3 0.3 convolution_bitcast_fusion
  57.7 0.3 copy-done.6
  58.2 1.2 %pad_maximum_fusion = f32[1536,256]{1,0:T(8,128)} fusion(f32[768,256]{1,0:T(8,128)S(1)} %bitcast.78, f32[256,256]{1,0:T(8,128)S(1)} %copy-done.8, f32[256,256]{1,0:T(8,128)S(1)} %copy-done.7, f32[256,256]{1,0:T(8,128)S(1)} %copy-done.6), kind=kLoop, calls=%fused_computation | loop fusion | flops 1179648 | bytes 3145728 | tf_op jit(solution)/shard_map/concatenate | solution.py:693
  59.4 0.9 fusion.2
  60.4 0.9 convert_select_fusion.1
  61.3 0.5 select_reduce_fusion
  62.1 1.1 %copy-done.2 = bf16[6,512,256]{2,1,0:T(8,128)(2,1)} copy-done((bf16[6,512,256]{2,1,0:T(8,128)(2,1)}, bf16[6,512,256]{2,1,0:T(8,128)(2,1)S(1)}, u32[]{:S(2)}) %copy-start.2) | copy-done | bytes 1572888
  63.2 35.9 %reduce.1 = (bf16[512,256]{1,0:T(8,128)(2,1)}, bf16[2,8,96,256]{3,2,1,0:T(8,128)(2,1)}) custom-call(bf16[6,512,256]{2,1,0:T(8,128)(2,1)} %copy-done.2, f32[512,256]{1,0:T(8,128)} %get-tuple-element.35.base_ref, f32[2,8,96,256]{3,2,1,0:T(8,128)} %bitcast.76), custom_call_target="tpu_custom_call" | custom-call | tf_op jit(solution)/shard_map/reduce/pallas_call | solution.py:593
  99.1 1.3 %convert_multiply_fusion = f32[2,8,96,256]{3,2,1,0:T(8,128)S(1)} fusion(bf16[2,8,96,256]{3,2,1,0:T(8,128)(2,1)} %get-tuple-element.41), kind=kLoop, calls=%fused_computation.1 | loop fusion | flops 786432 | bytes 2359296 | tf_op jit(solution)/shard_map/mul | solution.py:699
  100.4 0.9 slice.80
  101.4 0.9 fusion.11
  102.3 0.7 copy.24
  (34 shorter events, 0.4 us)
Async XLA Ops:
  24.1 31.1 %copy-start.11 = (s32[1,2]{1,0:T(1,128)S(1)}, s32[1,2]{1,0:T(1,128)}, u32[]{:S(2)}) copy-start(s32[1,2]{1,0:T(1,128)} %param.11) | copy-start | bytes 28
  24.1 31.1 %copy-start.1 = (bf16[512,256]{1,0:T(8,128)(2,1)S(1)}, bf16[512,256]{1,0:T(8,128)(2,1)}, u32[]{:S(2)}) copy-start(bf16[512,256]{1,0:T(8,128)(2,1)} %get-tuple-element.39) | copy-start | bytes 786436
  52.7 3.8 %copy-start = (bf16[512,256]{1,0:T(8,128)(2,1)S(1)}, bf16[512,256]{1,0:T(8,128)(2,1)}, u32[]{:S(2)}) copy-start(bf16[512,256]{1,0:T(8,128)(2,1)} %get-tuple-element.32) | copy-start | bytes 786436
  52.7 4.1 %copy-start.3 = (bf16[3,256,256]{2,1,0:T(8,128)(2,1)S(1)}, bf16[3,256,256]{2,1,0:T(8,128)(2,1)}, u32[]{:S(2)}) copy-start(bf16[3,256,256]{2,1,0:T(8,128)(2,1)} %taps_ref.1) | copy-start | bytes 1179652
  52.7 4.1 %copy-start.5 = (f32[512,256]{1,0:T(8,128)S(1)}, f32[512,256]{1,0:T(8,128)}, u32[]{:S(2)}) copy-start(f32[512,256]{1,0:T(8,128)} %get-tuple-element.31) | copy-start | bytes 1572868
  53.6 2.9 %collective-permute-start = (bf16[1,64,256]{2,1,0:T(8,128)(2,1)S(1)}, bf16[1,64,256]{2,1,0:T(8,128)(2,1)S(1)}, u32[]{:S(2)}, u32[]{:S(2)}) collective-permute-start(bf16[1,64,256]{2,1,0:T(8,128)(2,1)S(1)} %select_bitcast_fusion), channel_id=1, source_target_pairs={{0,1},{1,0},{2,3},{3,2},{4,5},{5,4},{6,7},{7,6},{8,9},{9,8},{10,11... | collective-permute-start | bytes 98312 | tf_op jit(solution)/shard_map/ppermute | solution.py:617
  55.0 5.4 %collective-permute-start.1 = (bf16[2,2,64,256]{3,2,1,0:T(8,128)(2,1)S(1)}, bf16[2,2,64,256]{3,2,1,0:T(8,128)(2,1)}, u32[]{:S(2)}, u32[]{:S(2)}) collective-permute-start(bf16[2,2,64,256]{3,2,1,0:T(8,128)(2,1)S(1)} %fusion.4), channel_id=1, source_target_pairs={{0,1},{1,0},{2,3},{3,2},{4,5},{5,4},{6,7},{7,6},{8,9},{9,8},{10,11... | collective-permute-start | bytes 393224 | tf_op jit(solution)/shard_map/ppermute | solution.py:617
  57.1 1.0 copy-start.6
  57.1 1.0 copy-start.7
  57.1 1.1 %copy-start.8 = (f32[256,256]{1,0:T(8,128)S(1)}, f32[256,256]{1,0:T(8,128)}, u32[]{:S(2)}) copy-start(f32[256,256]{1,0:T(8,128)} %get-tuple-element.38) | copy-start | bytes 786436
  58.2 1.3 %copy-start.10 = (f32[1,256]{1,0:T(1,128)S(1)}, f32[1,256]{1,0:T(1,128)}, u32[]{:S(2)}) copy-start(f32[1,256]{1,0:T(1,128)} %get-tuple-element.33) | copy-start | bytes 3076
  59.4 1.9 %copy-start.4 = (f32[2,768,256]{2,1,0:T(8,128)S(1)}, f32[2,768,256]{2,1,0:T(8,128)}, u32[]{:S(2)}) copy-start(f32[2,768,256]{2,1,0:T(8,128)} %get-tuple-element.34) | copy-start | bytes 4718596
  62.1 1.2 %copy-start.2 = (bf16[6,512,256]{2,1,0:T(8,128)(2,1)}, bf16[6,512,256]{2,1,0:T(8,128)(2,1)S(1)}, u32[]{:S(2)}) copy-start(bf16[6,512,256]{2,1,0:T(8,128)(2,1)S(1)} %bitcast_dynamic-update-slice_fusion.out_ref) | copy-start | bytes 4718596
  100.4 1.8 %copy-start.9 = (bf16[512,256]{1,0:T(8,128)(2,1)S(1)}, bf16[512,256]{1,0:T(8,128)(2,1)}, u32[]{:S(2)}) copy-start(bf16[512,256]{1,0:T(8,128)(2,1)} %get-tuple-element.40) | copy-start | bytes 786436

commit v5 on v4

--- a/solution.py
+++ b/solution.py
@@ -413,7 +413,8 @@
 
 def reduce_kernel(
     frames, out_ref, base_ref, w_ref, lat_ref, wsum_ref,
-    rb, sb, wp, ws, wr, ssem, rsem, ps, pr, rs_s, rs_r, ag_s, ag_r, fw_s, fw_r,
+    rb, sb, wp, ws, xr, wr, ssem, rsem, ps, pr, xs, xg,
+    rs_s, rs_r, ag_s, ag_r, px_s, px_r, fw_s, fw_r,
 ):
     f = lax.axis_index("frame")
     r = lax.axis_index("row")
@@ -429,15 +430,21 @@
 
     barrier = pltpu.get_barrier_semaphore()
     pl.semaphore_signal(barrier, inc=1, device_id=partner, device_id_type=MESH)
+    pl.semaphore_signal(barrier, inc=1, device_id=across, device_id_type=MESH)
+    deep = frames // 2
+    place = f // 2
+    mine = odd * deep
+    theirs = deep - mine
 
     def hello(k, carry):
         pl.semaphore_signal(
-            barrier, inc=1, device_id={"frame": lax.rem(f + k, frames)}, device_id_type=MESH
+            barrier, inc=1, device_id={"frame": 2 * lax.rem(place + k, deep) + odd},
+            device_id_type=MESH,
         )
         return carry
 
-    lax.fori_loop(1, frames, hello, 0)
-    pl.semaphore_wait(barrier, frames)
+    lax.fori_loop(1, deep, hello, 0)
+    pl.semaphore_wait(barrier, deep + 1)
 
     step = tokens // CHUNKS
     sent = (hi2, lo2, always, hi4, lo4, side)
@@ -469,30 +476,43 @@
             rb[kind, :, :] = jnp.zeros((tokens, rb.shape[2]), BF)
 
     halves.wait()
-    ws[...] = (w_ref[r] + wp[...]).astype(BF)
-
-    def piece(ref, mine, other, target, s_sem, r_sem, slot, k):
+    other_side = pl.ds(theirs, deep)
+    own_side = pl.ds(mine, deep)
+    ws[other_side] = (w_ref[r, other_side] + wp[other_side]).astype(BF)
+    swap = pltpu.make_async_remote_copy(
+        ws.at[other_side], xr, xs, xg, device_id=across, device_id_type=MESH
+    )
+    swap.start()
+
+    def column(index, source, target, s_sem, r_sem, k, slot):
         return pltpu.make_async_remote_copy(
-            mine, other, s_sem.at[k], r_sem.at[slot],
-            device_id={"frame": target}, device_id_type=MESH,
+            source, target, s_sem.at[k], r_sem.at[slot],
+            device_id={"frame": 2 * index + odd}, device_id_type=MESH,
         )
 
     def scatter(k):
-        target = lax.rem(f + k, frames)
-        return piece(ws, ws.at[target], wr.at[f], target, rs_s, rs_r, f, k)
+        index = lax.rem(place + k, deep)
+        return column(index, ws.at[mine + index], wr.at[place], rs_s, rs_r, k, place)
 
     def arrived(k):
-        source = lax.rem(f - k + frames, frames)
-        return source, piece(ws, ws.at[source], wr.at[source], source, rs_s, rs_r, source, k)
+        index = lax.rem(place - k + deep, deep)
+        return index, column(index, ws.at[mine + index], wr.at[index], rs_s, rs_r, k, index)
 
     def gather(k):
-        target = lax.rem(f + k, frames)
-        return piece(ws, wsum_ref.at[r, f], wsum_ref.at[r, f], target, ag_s, ag_r, f, k)
+        index = lax.rem(place + k, deep)
+        block = wsum_ref.at[r, mine + place]
+        return column(index, block, block, ag_s, ag_r, k, place)
 
     def gathered(k):
-        source = lax.rem(f - k + frames, frames)
-        return source, piece(
-            ws, wsum_ref.at[r, source], wsum_ref.at[r, source], source, ag_s, ag_r, source, k
+        index = lax.rem(place - k + deep, deep)
+        block = wsum_ref.at[r, mine + index]
+        return index, column(index, block, block, ag_s, ag_r, k, index)
+
+    def cross(side, index):
+        block = wsum_ref.at[r, side + index]
+        return pltpu.make_async_remote_copy(
+            block, block, px_s.at[index], px_r.at[index],
+            device_id=across, device_id_type=MESH,
         )
 
     def forward(j, own):
@@ -502,11 +522,13 @@
         )
 
     def run(body):
-        lax.fori_loop(1, frames, lambda k, carry: (body(k), carry)[1], 0)
-
-    run(lambda k: scatter(k).start())
+        lax.fori_loop(1, deep, lambda k, carry: (body(k), carry)[1], 0)
+
     for c in range(CHUNKS):
         copy(2, c, out_ref.at[2]).start()
+    swap.wait()
+    ws[own_side] = (w_ref[r, own_side] + wp[own_side] + xr[...].astype(F32)).astype(BF)
+    run(lambda k: scatter(k).start())
 
     even = jnp.where(odd == 0, 1.0, 0.0).astype(F32)
     for c in range(CHUNKS):
@@ -538,10 +560,14 @@
         waiting.wait_recv()
         return total + wr[source].astype(F32)
 
-    total = lax.fori_loop(1, frames, add_piece, w_ref[r, f] + wp[f])
-    wsum_ref[r, f] = total.astype(BF)
+    here = mine + place
+    total = lax.fori_loop(
+        1, deep, add_piece, w_ref[r, here] + wp[here] + xr[place].astype(F32)
+    )
+    wsum_ref[r, here] = total.astype(BF)
     run(lambda k: gather(k).start())
-    forward(f, r).start()
+    cross(mine, place).start()
+    forward(here, r).start()
 
     for c in range(CHUNKS):
         part = slice(c * step, (c + 1) * step)
@@ -559,17 +585,31 @@
         ).astype(BF)
 
     def pass_on(k):
-        source, waiting = gathered(k)
+        index, waiting = gathered(k)
         waiting.wait_recv()
-        forward(source, r).start()
+        cross(mine, index).start()
+        forward(mine + index, r).start()
 
     run(pass_on)
+
+    def crossed(index, carry):
+        cross(theirs, index).wait_recv()
+        forward(theirs + index, r).start()
+        return carry
+
+    lax.fori_loop(0, deep, crossed, 0)
 
     def finish(k):
         scatter(k).wait_send()
         gather(k).wait_send()
 
     run(finish)
+
+    def done(index, carry):
+        cross(mine, index).wait_send()
+        return carry
+
+    lax.fori_loop(0, deep, done, 0)
 
     def last(j, carry):
         forward(j, r).wait_send()
@@ -603,10 +643,11 @@
             pltpu.VMEM((2, count, width), BF),
             pltpu.VMEM(pieces, F32),
             pltpu.VMEM(pieces, BF),
-            pltpu.VMEM(pieces, BF),
-            dma((6, CHUNKS)), dma((6, CHUNKS)), dma(()), dma(()),
-            dma((frames,)), dma((frames,)), dma((frames,)), dma((frames,)),
-            dma((frames,)), dma((frames,)),
+            pltpu.VMEM((frames // 2,) + pieces[1:], BF),
+            pltpu.VMEM((frames // 2,) + pieces[1:], BF),
+            dma((6, CHUNKS)), dma((6, CHUNKS)), dma(()), dma(()), dma(()), dma(()),
+            dma((frames // 2,)), dma((frames // 2,)), dma((frames // 2,)), dma((frames // 2,)),
+            dma((frames // 2,)), dma((frames // 2,)), dma((frames,)), dma((frames,)),
         ],
         compiler_params=pltpu.CompilerParams(collective_id=1, has_side_effects=True),
         name="reduce",

time: 103 us -> 105 us (1.019)
  Pallas kernels: 85.3 us -> 87 us
    pallas_call x1, Pallas kernels: 35.9 us -> 37.6 us  [reduce(): pl.pallas_call(functools.partial(reduce_kernel, frames), out_shape=(jax.S...]
where the time goes in v5:
time: 105 us
  Pallas kernels  87 us (83%)
  other arithmetic  7.33 us (7%)
  local copies, waits for them, and re-layouts  4.36 us (4%)
  matrix products  3.14 us (3%)
  between operations  2.23 us (2%)
    pallas_call x1, Pallas kernels, reduce(): pl.pallas_call(functools.partial(reduce_kernel, frames), out_shape=(jax.S...  37.6 us
    pallas_call x1, Pallas kernels, attention(): pl.pallas_call(attention_kernel, out_shape=(full, jax.ShapeDtypeStruct((t...  28.5 us
    pallas_call x1, Pallas kernels, fetch(): pl.pallas_call(functools.partial(fetch_kernel, frames), out_shape=(jax.Sh...  20.9 us
    dot_general x6, matrix products, mm(): lax.dot_general(a, b, (((ca,), (cb,)), ((), ())), preferred_element_type=...  3.14 us
    unnamed x30, local copies, waits for them, and re-layouts  2.51 us
  transfers between devices with their start and end apart: 2, of which 0 were waited for; matrix products, arithmetic and copies ran while one was open for 5% of the time, Pallas kernels for 0%

profile of v5, /device:TPU:0, one launch (start us, length us, event | category | flops | bytes accessed | tf_op | source)
XLA Modules:
  0.0 104.7 jit_solution(9781157713195675338)
XLA Ops:
  1.9 0.7 select_select_fusion
  2.6 0.6 pad_add_fusion.meta_ref
  3.2 20.9 %fetch.1 = (bf16[6,512,256]{2,1,0:T(8,128)(2,1)}, bf16[6,128,256]{2,1,0:T(8,128)(2,1)}, bf16[512,256]{1,0:T(8,128)(2,1)}, bf16[256,512]{1,0:T(8,128)(2,1)}, bf16...) custom-call(s32[1]{0:T(128)S(6)} %copy.23.level_ref, ...), custom_call_target="tpu_custom_call" | custom-call | tf_op jit(solution)/shard_map/fetch/pallas_call | solution.py:393
  24.1 28.5 %attention.1 = (f32[512,256]{1,0:T(8,128)}, bf16[512,256]{1,0:T(8,128)(2,1)}, f32[512,256]{1,0:T(8,128)}, f32[2,768,256]{2,1,0:T(8,128)}, f32[256,256]{1,0:T(8,1...) custom-call(s32[5]{0:T(128)} %pad_add_fusion.meta_ref, bf16[6,512,256]{2,1,0:T(8,128)(2,1)} %get-tuple-element.24.buf_hbm, ...), custom_call_target="tpu_custom_call" | custom-call | flops 20000000000 | bytes 8000000 | tf_op jit(solution)/shard_map/attention/pallas_call | solution.py:189
  52.7 0.9 select_bitcast_fusion
  53.6 0.3 collective-permute-start
  53.9 1.1 %fusion.4 = bf16[2,2,64,256]{3,2,1,0:T(8,128)(2,1)S(1)} fusion(f32[2,12,64,256]{3,2,1,0:T(8,128)} %bitcast.84, pred[]{:T(512)S(6)} %eq.115), kind=kLoop, calls=%fused_computation.23 | loop fusion | flops 65536 | bytes 393217 | tf_op jit(solution)/shard_map/convert_element_type | solution.py:712
  55.0 0.2 collective-permute-start.1
  55.2 1.2 %convolution_bitcast_fusion.1 = f32[1,256,256]{2,1,0:T(8,128)S(1)} fusion(bf16[512,256]{1,0:T(8,128)(2,1)} %get-tuple-element.32, bf16[512,256]{1,0:T(8,128)(2,1)S(1)} %copy-done.1), kind=kOutput, calls=%fused_computation.8 | convolution fusion | flops 67108864 | bytes 786432 | tf_op jit(solution)/shard_map/dot_general | solution.py:24
  56.5 0.3 convolution_bitcast_fusion.2
  56.8 0.2 convolution_add_fusion.2
  57.1 0.2 convolution_add_fusion.1
  57.3 0.3 convolution_bitcast_fusion
  57.7 0.3 copy-done.6
  58.2 1.2 %pad_maximum_fusion = f32[1536,256]{1,0:T(8,128)} fusion(f32[768,256]{1,0:T(8,128)S(1)} %bitcast.78, f32[256,256]{1,0:T(8,128)S(1)} %copy-done.8, f32[256,256]{1,0:T(8,128)S(1)} %copy-done.7, f32[256,256]{1,0:T(8,128)S(1)} %copy-done.6), kind=kLoop, calls=%fused_computation | loop fusion | flops 1179648 | bytes 3145728 | tf_op jit(solution)/shard_map/concatenate | solution.py:734
  59.4 0.9 fusion.2
  60.4 0.9 convert_select_fusion.1
  61.3 0.5 select_reduce_fusion
  62.1 1.1 %copy-done.2 = bf16[6,512,256]{2,1,0:T(8,128)(2,1)} copy-done((bf16[6,512,256]{2,1,0:T(8,128)(2,1)}, bf16[6,512,256]{2,1,0:T(8,128)(2,1)S(1)}, u32[]{:S(2)}) %copy-start.2) | copy-done | bytes 1572888
  63.2 37.6 %reduce.1 = (bf16[512,256]{1,0:T(8,128)(2,1)}, bf16[2,8,96,256]{3,2,1,0:T(8,128)(2,1)}) custom-call(bf16[6,512,256]{2,1,0:T(8,128)(2,1)} %copy-done.2, f32[512,256]{1,0:T(8,128)} %get-tuple-element.35.base_ref, f32[2,8,96,256]{3,2,1,0:T(8,128)} %bitcast.76), custom_call_target="tpu_custom_call" | custom-call | tf_op jit(solution)/shard_map/reduce/pallas_call | solution.py:633
  100.8 1.3 %convert_multiply_fusion = f32[2,8,96,256]{3,2,1,0:T(8,128)S(1)} fusion(bf16[2,8,96,256]{3,2,1,0:T(8,128)(2,1)} %get-tuple-element.41), kind=kLoop, calls=%fused_computation.1 | loop fusion | flops 786432 | bytes 2359296 | tf_op jit(solution)/shard_map/mul | solution.py:740
  102.1 0.9 slice.80
  103.1 0.9 fusion.11
  104.0 0.7 copy.24
  (34 shorter events, 0.4 us)
Async XLA Ops:
  24.1 31.1 %copy-start.11 = (s32[1,2]{1,0:T(1,128)S(1)}, s32[1,2]{1,0:T(1,128)}, u32[]{:S(2)}) copy-start(s32[1,2]{1,0:T(1,128)} %param.11) | copy-start | bytes 28
  24.1 31.1 %copy-start.1 = (bf16[512,256]{1,0:T(8,128)(2,1)S(1)}, bf16[512,256]{1,0:T(8,128)(2,1)}, u32[]{:S(2)}) copy-start(bf16[512,256]{1,0:T(8,128)(2,1)} %get-tuple-element.39) | copy-start | bytes 786436
  52.7 3.8 %copy-start = (bf16[512,256]{1,0:T(8,128)(2,1)S(1)}, bf16[512,256]{1,0:T(8,128)(2,1)}, u32[]{:S(2)}) copy-start(bf16[512,256]{1,0:T(8,128)(2,1)} %get-tuple-element.32) | copy-start | bytes 786436
  52.7 4.1 %copy-start.3 = (bf16[3,256,256]{2,1,0:T(8,128)(2,1)S(1)}, bf16[3,256,256]{2,1,0:T(8,128)(2,1)}, u32[]{:S(2)}) copy-start(bf16[3,256,256]{2,1,0:T(8,128)(2,1)} %taps_ref.1) | copy-start | bytes 1179652
  52.7 4.1 %copy-start.5 = (f32[512,256]{1,0:T(8,128)S(1)}, f32[512,256]{1,0:T(8,128)}, u32[]{:S(2)}) copy-start(f32[512,256]{1,0:T(8,128)} %get-tuple-element.31) | copy-start | bytes 1572868
  53.6 2.9 %collective-permute-start = (bf16[1,64,256]{2,1,0:T(8,128)(2,1)S(1)}, bf16[1,64,256]{2,1,0:T(8,128)(2,1)S(1)}, u32[]{:S(2)}, u32[]{:S(2)}) collective-permute-start(bf16[1,64,256]{2,1,0:T(8,128)(2,1)S(1)} %select_bitcast_fusion), channel_id=1, source_target_pairs={{0,1},{1,0},{2,3},{3,2},{4,5},{5,4},{6,7},{7,6},{8,9},{9,8},{10,11... | collective-permute-start | bytes 98312 | tf_op jit(solution)/shard_map/ppermute | solution.py:658
  55.0 5.4 %collective-permute-start.1 = (bf16[2,2,64,256]{3,2,1,0:T(8,128)(2,1)S(1)}, bf16[2,2,64,256]{3,2,1,0:T(8,128)(2,1)}, u32[]{:S(2)}, u32[]{:S(2)}) collective-permute-start(bf16[2,2,64,256]{3,2,1,0:T(8,128)(2,1)S(1)} %fusion.4), channel_id=1, source_target_pairs={{0,1},{1,0},{2,3},{3,2},{4,5},{5,4},{6,7},{7,6},{8,9},{9,8},{10,11... | collective-permute-start | bytes 393224 | tf_op jit(solution)/shard_map/ppermute | solution.py:658
  57.1 1.0 copy-start.6
  57.1 1.0 copy-start.7
  57.1 1.1 %copy-start.8 = (f32[256,256]{1,0:T(8,128)S(1)}, f32[256,256]{1,0:T(8,128)}, u32[]{:S(2)}) copy-start(f32[256,256]{1,0:T(8,128)} %get-tuple-element.38) | copy-start | bytes 786436
  58.2 1.3 %copy-start.10 = (f32[1,256]{1,0:T(1,128)S(1)}, f32[1,256]{1,0:T(1,128)}, u32[]{:S(2)}) copy-start(f32[1,256]{1,0:T(1,128)} %get-tuple-element.33) | copy-start | bytes 3076
  59.4 1.9 %copy-start.4 = (f32[2,768,256]{2,1,0:T(8,128)S(1)}, f32[2,768,256]{2,1,0:T(8,128)}, u32[]{:S(2)}) copy-start(f32[2,768,256]{2,1,0:T(8,128)} %get-tuple-element.34) | copy-start | bytes 4718596
  62.1 1.2 %copy-start.2 = (bf16[6,512,256]{2,1,0:T(8,128)(2,1)}, bf16[6,512,256]{2,1,0:T(8,128)(2,1)S(1)}, u32[]{:S(2)}) copy-start(bf16[6,512,256]{2,1,0:T(8,128)(2,1)S(1)} %bitcast_dynamic-update-slice_fusion.out_ref) | copy-start | bytes 4718596
  102.1 1.8 %copy-start.9 = (bf16[512,256]{1,0:T(8,128)(2,1)S(1)}, bf16[512,256]{1,0:T(8,128)(2,1)}, u32[]{:S(2)}) copy-start(bf16[512,256]{1,0:T(8,128)(2,1)} %get-tuple-element.40) | copy-start | bytes 786436
